TPU v7x, 128 devices: a whole 4x4x4 slice. The times are simulated.
128 devices in a mesh: brick: 8 (over x, core), dom: 16 (over z, y).
Axes of the slice: x: 4, y: 4, z: 4, core: 2. Of those that a mesh axis runs over, the one named last changes fastest.
Arguments:
- velocity: bfloat16 [3, 27, 131072], P(None, None, ('brick', 'dom')), may hold values from -6 to 6
- adjoint: bfloat16 [3, 27, 131072], P(None, None, ('brick', 'dom')), may hold values from -6 to 6
- coupling: bfloat16 [27, 27], replicated, may hold values from -1.25 to 1.25
- jac_weight: float32 [131072], P(('brick', 'dom')), may hold values from 0.25 to 4
- owner: int32 [131072, 1], P(('brick', 'dom')), may hold values from 0 to 127; in each aligned block of 1024 rows (0 to 1023, 1024 to 2047, ...) at most 16 rows name the same one
- local_block: int32 [131072], P(('brick', 'dom')), may hold values from 0 to 4095
- offsets: int32 [128, 131072], P(None, ('brick', 'dom')), may hold values from 0 to 127
- margin: float32 [128, 131072], P(None, ('brick', 'dom')), may hold values from 0.002 to 0.02
- filtered: float32 [512, 1024, 128], P('brick', 'dom'), may hold values from 0 to 1
Outputs:
- sensitivity: float32 [512, 1024, 128], P('brick', 'dom')
- elem_density: float32 [131072], P(('brick', 'dom'))
Inputs may be any that keep to these rules, and one draw needn't show every extreme that they name: Among the 1024 elements of one device at most 16 have the same owner, and exactly 16 for some owner.
All inputs are finite; a program needn't handle non-finite values.
Results may differ from a plain program's by a relative error of at most 0.0003.
Values sent between devices are 32-bit elements; how exact they have to be, the bound alone decides.
A program may use at most 64 MiB of HBM per device.

v0:
```python
import jax
import jax.numpy as jnp
from jax import lax
from jax.sharding import PartitionSpec as P

GZ = 128


sharpness = 8.0
threshold = 0.5
ramp_q = 0.1
radius_sq = 1.5
relax = 0.9


def padded(cells, sides, width):
    for axis, dim in sides:
        count = lax.axis_size(axis)
        ends = count - 1
        head = lax.slice_in_dim(cells, 0, width, axis=dim)
        tail = lax.slice_in_dim(cells, cells.shape[dim] - width, cells.shape[dim], axis=dim)
        cells = jnp.concatenate(
            [
                lax.ppermute(tail, axis, [(i, (i + 1) % count) for i in range(ends)]),
                cells,
                lax.ppermute(head, axis, [((i + 1) % count, i) for i in range(ends)]),
            ],
            axis=dim,
        )
    return cells


def project(field):
    base = jnp.tanh(sharpness * threshold)
    return (base + jnp.tanh(sharpness * (field - threshold))) / (
        base + jnp.tanh(sharpness * (1.0 - threshold))
    )


def projection_slope(field):
    base = jnp.tanh(sharpness * threshold)
    tangent = jnp.tanh(sharpness * (field - threshold))
    return sharpness * (1.0 - tangent * tangent) / (base + jnp.tanh(sharpness * (1.0 - threshold)))


def ramp_slope(density):
    return -ramp_q * (1.0 + ramp_q) / ((ramp_q + density) * (ramp_q + density))


def margin_rows(offsets, margin):
    entries, count = offsets.shape
    group = min(256, count)
    blocks = count // group
    lanes = jnp.arange(GZ, dtype=jnp.int32)
    grouped_offsets = offsets.reshape(entries, blocks, group).transpose(1, 0, 2)
    grouped_margin = margin.reshape(entries, blocks, group).transpose(1, 0, 2)

    def one_block(pair):
        block_offsets, block_margin = pair
        hits = block_offsets[:, :, None] == lanes[None, None, :]
        return jnp.sum(jnp.where(hits, block_margin[:, :, None], jnp.float32(0.0)), axis=0)

    return lax.map(one_block, (grouped_offsets, grouped_margin)).reshape(count, GZ)


def jacobi_extended(extended, source):
    padded_z = jnp.pad(extended, ((0, 0), (0, 0), (1, 1)))
    middle = extended[1:-1, 1:-1]
    near = extended[2:, 1:-1] + extended[:-2, 1:-1]
    near = near + extended[1:-1, 2:] + extended[1:-1, :-2]
    near = near + padded_z[1:-1, 1:-1, 2:] + padded_z[1:-1, 1:-1, :-2]
    center = 1.0 + 6.0 * radius_sq
    return middle + relax * (source - (center * middle - radius_sq * near)) / center


def with_rim(field):
    return padded(field, (("brick", 0), ("dom", 1)), 1)


def body(velocity, adjoint, coupling, jac_weight, owner, local_block, offsets, margin, filtered):
    brick_count = lax.axis_size("brick")
    dom_count = lax.axis_size("dom")
    device_count = brick_count * dom_count
    element_count = owner.shape[0]
    width_x, width_y, depth = filtered.shape
    capacity = max(2, 2 * element_count // device_count)
    target = owner[:, 0]
    matches = (target[:, None] == jnp.arange(device_count, dtype=jnp.int32)[None, :]).astype(
        jnp.int32
    )
    position = jnp.sum(jnp.cumsum(matches, axis=0) * matches, axis=1) - 1
    placed = target * capacity + position
    voxel_rows = project(filtered).reshape(width_x * width_y, depth)
    weights = margin_rows(offsets, margin)
    mixed = jnp.einsum("ij,cje->cie", coupling, adjoint, preferred_element_type=jnp.float32)
    products = jac_weight * jnp.sum(velocity.astype(jnp.float32) * mixed, axis=(0, 1))
    requests = jnp.full((device_count * capacity,), -1, jnp.int32).at[placed].set(local_block)
    requests = requests.reshape(device_count, capacity)
    asked = lax.all_to_all(requests, ("brick", "dom"), split_axis=0, concat_axis=0, tiled=True)
    present = (asked >= 0).astype(jnp.float32)
    found = jnp.take(voxel_rows, jnp.maximum(asked, 0), axis=0) * present[..., None]
    returned = lax.all_to_all(found, ("brick", "dom"), split_axis=0, concat_axis=0, tiled=True)
    own_rows = returned.reshape(device_count * capacity, depth)[placed]
    density = jnp.sum(weights * own_rows, axis=1)
    terms = ramp_slope(density) * products
    outgoing = (
        jnp.zeros((device_count * capacity, depth), jnp.float32)
        .at[placed]
        .set(terms[:, None] * weights)
    )
    arrived = lax.all_to_all(
        outgoing.reshape(device_count, capacity, depth),
        ("brick", "dom"),
        split_axis=0,
        concat_axis=0,
        tiled=True,
    )
    arrived = arrived.reshape(device_count * capacity, depth)
    selector = (
        asked.reshape(1, -1) == jnp.arange(width_x * width_y, dtype=jnp.int32)[:, None]
    ).astype(jnp.float32)
    summed = jnp.dot(
        selector, arrived, precision=lax.Precision.HIGHEST, preferred_element_type=jnp.float32
    )
    source = summed.reshape(width_x, width_y, depth) * projection_slope(filtered)
    first = jacobi_extended(with_rim(source), source)
    result = jacobi_extended(with_rim(first), source)
    return (result, density)


def solution(mesh):
    return jax.shard_map(
        body,
        mesh=mesh,
        in_specs=(
            P(None, None, ("brick", "dom")),
            P(None, None, ("brick", "dom")),
            P(),
            P(("brick", "dom")),
            P(("brick", "dom"), None),
            P(("brick", "dom")),
            P(None, ("brick", "dom")),
            P(None, ("brick", "dom")),
            P("brick", "dom", None),
        ),
        out_specs=(P("brick", "dom", None), P(("brick", "dom"))),
        check_vma=False,
    )
```

profile of v0, /device:TPU:1, one launch (start us, length us, event | category | flops | bytes accessed | tf_op | source)
XLA Modules:
  0.0 195.1 jit_solution(13145821379865048431)
XLA Ops:
  2.3 4.5 %scatter_custom_fusion = s32[2048]{0:T(1024)S(1)} fusion(s32[1024]{0:T(1024)S(1)} %bitcast.72, s32[1024]{0:T(1024)} %param.16, s32[]{:T(128)} %constant.36.clone.1), kind=kCustom, calls=%fused_computation.95 | custom fusion | bytes 8704 | tf_op jit(solution)/shard_map/scatter | solution.py:97
  7.5 11.5 %all-to-all-start = ((s32[128,1,16]{2,1,0:T(1,128)}), s32[128,1,16]{2,1,0:T(1,128)S(1)}, u32[]{:S(2)}, u32[]{:S(2)}) async-start(s32[128,1,16]{2,1,0:T(1,128)} %bitcast.7), calls=%async_computation | async-start | bytes 131072 | tf_op jit(solution)/shard_map/all_to_all | solution.py:99
  23.1 5.6 %all-to-all-done = s32[128,1,16]{2,1,0:T(1,128)S(1)} async-done(((s32[128,1,16]{2,1,0:T(1,128)}), s32[128,1,16]{2,1,0:T(1,128)S(1)}, u32[]{:S(2)}, u32[]{:S(2)}) %all-to-all-start) | async-done | bytes 8224 | tf_op jit(solution)/shard_map/all_to_all | solution.py:99
  29.2 5.5 %gather_fusion = f32[2048,128]{1,0:T(8,128)S(1)} fusion(f32[4096,128]{1,0:T(8,128)S(1)} %bitcast.60, s32[2048]{0:T(1024)S(1)} %broadcast_clamp_fusion), kind=kCustom, calls=%fused_computation | custom fusion | bytes 2105344 | tf_op jit(solution)/shard_map/jit(_take)/gather | solution.py:101
  36.2 4.3 %all-to-all-start.1 = ((f32[128,16,128]{2,1,0:T(8,128)}), f32[128,16,128]{2,1,0:T(8,128)S(1)}, u32[]{:S(2)}, u32[]{:S(2)}) async-start(f32[128,16,128]{2,1,0:T(8,128)} %select_multiply_fusion), calls=%async_computation.1 | async-start | bytes 2097152 | tf_op jit(solution)/shard_map/all_to_all | solution.py:102
  40.6 52.6 %while.11 = (s32[]{:T(128)}, f32[4,256,128]{2,1,0:T(8,128)S(1)}, s32[4,128,256]{1,2,0:T(8,128)}, f32[4,128,256]{1,2,0:T(8,128)}, s32[]{:T(128)}) while((s32[]{:T(128)}, f32[4,256,128]{2,1,0:T(8,128)S(1)}, s32[4,128,256]{1,2,0:T(8,128)}, f32[4,128,256]{1,2,0:T(8,128)}, s32[]{:T(128)}) %tuple.39), condition=%wide.region_6.7_spmd.clone, body=%wide.region_4.6_spmd.clone.sunk | while | flops 12550146 | bytes 1704017 | solution.py:63
  42.7 11.0 %select_reduce_fusion.2 = f32[256,128]{1,0:T(8,128)S(1)} fusion(f32[128,256]{1,0:T(8,128)S(1)} %bitcast.62, s32[128,256]{1,0:T(8,128)S(1)} %bitcast.63), kind=kLoop, calls=%fused_computation.6.clone.1 | loop fusion | flops 12550144 | bytes 393216 | tf_op jit(solution)/shard_map/while/body/eval_jaxpr/reduce_sum | solution.py:61
  55.8 11.0 %select_reduce_fusion.2 = f32[256,128]{1,0:T(8,128)S(1)} fusion(f32[128,256]{1,0:T(8,128)S(1)} %bitcast.62, s32[128,256]{1,0:T(8,128)S(1)} %bitcast.63), kind=kLoop, calls=%fused_computation.6.clone.1 | loop fusion | flops 12550144 | bytes 393216 | tf_op jit(solution)/shard_map/while/body/eval_jaxpr/reduce_sum | solution.py:61
  68.9 11.0 %select_reduce_fusion.2 = f32[256,128]{1,0:T(8,128)S(1)} fusion(f32[128,256]{1,0:T(8,128)S(1)} %bitcast.62, s32[128,256]{1,0:T(8,128)S(1)} %bitcast.63), kind=kLoop, calls=%fused_computation.6.clone.1 | loop fusion | flops 12550144 | bytes 393216 | tf_op jit(solution)/shard_map/while/body/eval_jaxpr/reduce_sum | solution.py:61
  82.1 11.0 %select_reduce_fusion.2 = f32[256,128]{1,0:T(8,128)S(1)} fusion(f32[128,256]{1,0:T(8,128)S(1)} %bitcast.62, s32[128,256]{1,0:T(8,128)S(1)} %bitcast.63), kind=kLoop, calls=%fused_computation.6.clone.1 | loop fusion | flops 12550144 | bytes 393216 | tf_op jit(solution)/shard_map/while/body/eval_jaxpr/reduce_sum | solution.py:61
  98.0 4.1 %scatter_custom_fusion.1 = f32[2048,128]{1,0:T(8,128)} fusion(s32[1024]{0:T(1024)S(1)} %bitcast.74, f32[1024,128]{1,0:T(8,128)S(1)} %bitcast_multiply_fusion, f32[]{:T(128)} %constant.67.clone.1), kind=kCustom, calls=%fused_computation.72 | custom fusion | bytes 1048580 | tf_op jit(solution)/shard_map/scatter | solution.py:109
  102.0 9.8 %all-to-all-start.2 = ((f32[128,16,128]{2,1,0:T(8,128)}), f32[128,16,128]{2,1,0:T(8,128)S(1)}, u32[]{:S(2)}, u32[]{:S(2)}) async-start(f32[128,16,128]{2,1,0:T(8,128)} %bitcast.21), calls=%async_computation.2 | async-start | bytes 2097152 | tf_op jit(solution)/shard_map/all_to_all | solution.py:111
  113.4 17.3 %all-to-all-done.2 = f32[128,16,128]{2,1,0:T(8,128)S(1)} async-done(((f32[128,16,128]{2,1,0:T(8,128)}), f32[128,16,128]{2,1,0:T(8,128)S(1)}, u32[]{:S(2)}, u32[]{:S(2)}) %all-to-all-start.2) | async-done | bytes 1048608 | tf_op jit(solution)/shard_map/all_to_all | solution.py:111
  130.7 16.5 %multiply_multiply_fusion = f32[64,64,128]{2,1,0:T(8,128)S(1)} fusion(f32[64,64,128]{2,1,0:T(8,128)S(1)} %copy-done.1, f32[2048,128,1]{1,0,2:T(8,128)S(1)} %bitcast.68, s32[64,64]{1,0:T(8,128)S(1)} %multiply_add_fusion, s32[2048]{0:T(1024)S(1)} %eq.74), kind=kOutput, calls=%fused_computation.61 | convolution fusion | flops 12896436224 | bytes 5267456 | tf_op jit(solution)/shard_map/dot_general | solution.py:122
  147.3 3.4 %collective-permute-start.1 = (f32[1,64,128]{2,1,0:T(8,128)S(1)}, f32[1,64,128]{2,1,0:T(8,128)S(1)}, u32[]{:S(2)}, u32[]{:S(2)}) collective-permute-start(f32[1,64,128]{2,1,0:T(8,128)S(1)} %get-tuple-element.70), channel_id=1, source_target_pairs={{0,16},{16,32},{32,48},{48,64},{64,80},{80,96},{96,112},{1,17},{17... | collective-permute-start | bytes 98312 | tf_op jit(solution)/shard_map/ppermute | solution.py:24
  152.6 3.3 %collective-permute-done = f32[1,64,128]{2,1,0:T(8,128)S(1)} collective-permute-done((f32[1,64,128]{2,1,0:T(8,128)S(1)}, f32[1,64,128]{2,1,0:T(8,128)S(1)}, u32[]{:S(2)}, u32[]{:S(2)}) %collective-permute-start) | collective-permute-done | bytes 32800 | tf_op jit(solution)/shard_map/ppermute | solution.py:26
  159.8 3.1 %collective-permute-done.2 = f32[66,1,128]{2,1,0:T(1,128)S(1)} collective-permute-done((f32[66,1,128]{2,1,0:T(1,128)S(1)}, f32[66,1,128]{2,1,0:T(1,128)S(1)}, u32[]{:S(2)}, u32[]{:S(2)}) %collective-permute-start.2) | collective-permute-done | bytes 33824 | tf_op jit(solution)/shard_map/ppermute | solution.py:26
  162.9 3.7 %select_maximum_fusion.4 = f32[66,66,130]{2,1,0:T(8,128)S(1)} fusion(f32[66,1,128]{2,1,0:T(1,128)S(1)} %collective-permute-done.2, f32[66,1,128]{2,1,0:T(1,128)S(1)} %collective-permute-done.3, f32[1,64,128]{2,1,0:T(8,128)S(1)} %collective-permute-done, f32[64,64,128]{2,1,0:T(8,128)S(1)} %multiply_multiply_fusion, f32[1,64,128]{2,1,0:T(8,128)S(1)} %collective-permute-done.1), kind=kLoop, calls=%fused_computation.20 | loop fusion | flops 6795360 | bytes 4495392 | tf_op jit(solution)/shard_map/concatenate | solution.py:22
  166.6 4.1 %fusion.19 = f32[64,64,128]{2,1,0:T(8,128)S(1)} fusion(f32[64,64,128]{2,1,0:T(8,128)S(1)} %multiply_multiply_fusion, f32[66,66,130]{2,1,0:T(8,128)S(1)} %select_maximum_fusion.4, f32[66,1,128]{2,1,0:T(1,128)S(1)} %collective-permute-done.3, f32[1,64,128]{2,1,0:T(8,128)S(1)} %collective-permute-done, f32[1,64,128]{2,1,0:T(8,128)S(1)} %collective-permute-done.1, ...), kind=kLoop, calls=%fused_computation.48 | loop fusion | flops 9961472 | bytes 8521728 | tf_op jit(solution)/shard_map/add | solution.py:73
  170.7 3.3 %collective-permute-start.5 = (f32[1,64,128]{2,1,0:T(8,128)S(1)}, f32[1,64,128]{2,1,0:T(8,128)S(1)}, u32[]{:S(2)}, u32[]{:S(2)}) collective-permute-start(f32[1,64,128]{2,1,0:T(8,128)S(1)} %get-tuple-element.68), channel_id=1, source_target_pairs={{0,16},{16,32},{32,48},{48,64},{64,80},{80,96},{96,112},{1,17},{17... | collective-permute-start | bytes 98312 | tf_op jit(solution)/shard_map/ppermute | solution.py:24
  176.0 3.3 %collective-permute-done.4 = f32[1,64,128]{2,1,0:T(8,128)S(1)} collective-permute-done((f32[1,64,128]{2,1,0:T(8,128)S(1)}, f32[1,64,128]{2,1,0:T(8,128)S(1)}, u32[]{:S(2)}, u32[]{:S(2)}) %collective-permute-start.4) | collective-permute-done | bytes 32800 | tf_op jit(solution)/shard_map/ppermute | solution.py:26
  182.3 3.9 %collective-permute-done.6 = f32[66,1,128]{2,1,0:T(1,128)S(1)} collective-permute-done((f32[66,1,128]{2,1,0:T(1,128)S(1)}, f32[66,1,128]{2,1,0:T(1,128)S(1)}, u32[]{:S(2)}, u32[]{:S(2)}) %collective-permute-start.6) | collective-permute-done | bytes 33824 | tf_op jit(solution)/shard_map/ppermute | solution.py:26
  186.2 3.7 %select_maximum_fusion = f32[66,66,130]{2,1,0:T(8,128)S(1)} fusion(f32[66,1,128]{2,1,0:T(1,128)S(1)} %collective-permute-done.6, f32[66,1,128]{2,1,0:T(1,128)S(1)} %collective-permute-done.7, f32[1,64,128]{2,1,0:T(8,128)S(1)} %collective-permute-done.4, f32[64,64,128]{2,1,0:T(8,128)S(1)} %fusion.19, f32[1,64,128]{2,1,0:T(8,128)S(1)} %collective-permute-done.5), kind=kLoop, calls=%fused_computation.16 | loop fusion | flops 6795360 | bytes 4495392 | tf_op jit(solution)/shard_map/concatenate | solution.py:22
  189.9 5.2 %fusion.11 = f32[64,64,128]{2,1,0:T(8,128)} fusion(f32[64,64,128]{2,1,0:T(8,128)S(1)} %fusion.19, f32[64,64,128]{2,1,0:T(8,128)S(1)} %multiply_multiply_fusion, f32[66,66,130]{2,1,0:T(8,128)S(1)} %select_maximum_fusion, f32[66,1,128]{2,1,0:T(1,128)S(1)} %collective-permute-done.7, f32[1,64,128]{2,1,0:T(8,128)S(1)} %collective-permute-done.4, ...), kind=kLoop, calls=%fused_computation.30 | loop fusion | flops 9961472 | bytes 10618880 | tf_op jit(solution)/shard_map/add | solution.py:73
  (92 shorter events, 33.5 us)
Async XLA Ops:
  0.6 92.5 %copy-start = (bf16[3,27,1024]{2,1,0:T(8,128)(2,1)S(1)}, bf16[3,27,1024]{2,1,0:T(8,128)(2,1)}, u32[]{:S(2)}) copy-start(bf16[3,27,1024]{2,1,0:T(8,128)(2,1)} %param.12) | copy-start | bytes 497668
  0.6 1.3 copy-start.6
  7.5 21.2 %all-to-all-start = ((s32[128,1,16]{2,1,0:T(1,128)}), s32[128,1,16]{2,1,0:T(1,128)S(1)}, u32[]{:S(2)}, u32[]{:S(2)}) async-start(s32[128,1,16]{2,1,0:T(1,128)} %bitcast.7), calls=%async_computation | async-start | bytes 131072 | tf_op jit(solution)/shard_map/all_to_all | solution.py:99
  19.0 2.1 %copy-start.4 = (s32[128,1024]{1,0:T(8,128)S(1)}, s32[128,1024]{1,0:T(8,128)}, u32[]{:S(2)}) copy-start(s32[128,1024]{1,0:T(8,128)} %param.17) | copy-start | bytes 1572868
  19.0 3.1 %copy-start.5 = (f32[128,1024]{1,0:T(8,128)S(1)}, f32[128,1024]{1,0:T(8,128)}, u32[]{:S(2)}) copy-start(f32[128,1024]{1,0:T(8,128)} %param.18) | copy-start | bytes 1572868
  34.7 5.8 %copy-start.2 = (f32[4,256,128]{2,1,0:T(8,128)S(1)}, f32[4,256,128]{2,1,0:T(8,128)}, u32[]{:S(2)}) copy-start(f32[4,256,128]{2,1,0:T(8,128)} %custom-call.4) | copy-start | bytes 1572868
  36.2 57.2 %all-to-all-start.1 = ((f32[128,16,128]{2,1,0:T(8,128)}), f32[128,16,128]{2,1,0:T(8,128)S(1)}, u32[]{:S(2)}, u32[]{:S(2)}) async-start(f32[128,16,128]{2,1,0:T(8,128)} %select_multiply_fusion), calls=%async_computation.1 | async-start | bytes 2097152 | tf_op jit(solution)/shard_map/all_to_all | solution.py:102
  40.5 52.7 %copy-start.9 = (bf16[3,27,1024]{2,1,0:T(8,128)(2,1)S(1)}, bf16[3,27,1024]{2,1,0:T(8,128)(2,1)}, u32[]{:S(2)}) copy-start(bf16[3,27,1024]{2,1,0:T(8,128)(2,1)} %param.11) | copy-start | bytes 497668
  40.5 52.6 %copy-start.10 = (bf16[27,27]{1,0:T(8,128)(2,1)S(1)}, bf16[27,27]{1,0:T(8,128)(2,1)}, u32[]{:S(2)}) copy-start(bf16[27,27]{1,0:T(8,128)(2,1)} %param.13) | copy-start | bytes 4378
  93.2 3.1 %copy-start.3 = (f32[4,256,128]{2,1,0:T(8,128)}, f32[4,256,128]{2,1,0:T(8,128)S(1)}, u32[]{:S(2)}) copy-start(f32[4,256,128]{2,1,0:T(8,128)S(1)} %get-tuple-element.29) | copy-start | bytes 1572868
  93.4 3.1 %copy-start.8 = (f32[1024]{0:T(1024)S(1)}, f32[1024]{0:T(1024)}, u32[]{:S(2)}) copy-start(f32[1024]{0:T(1024)} %param.14) | copy-start | bytes 12292
  96.5 5.5 %copy-start.7 = (f32[1,2,4,128]{3,1,2,0:T(2,128)}, f32[1,2,4,128]{3,1,2,0:T(2,128)S(1)}, u32[]{:S(2)}) copy-start(f32[1,2,4,128]{3,1,2,0:T(2,128)S(1)} %copy.51) | copy-start | bytes 12292
  96.6 34.2 %copy-start.1 = (f32[64,64,128]{2,1,0:T(8,128)S(1)}, f32[64,64,128]{2,1,0:T(8,128)}, u32[]{:S(2)}) copy-start(f32[64,64,128]{2,1,0:T(8,128)} %param.19) | copy-start | bytes 6291460
  102.0 28.7 %all-to-all-start.2 = ((f32[128,16,128]{2,1,0:T(8,128)}), f32[128,16,128]{2,1,0:T(8,128)S(1)}, u32[]{:S(2)}, u32[]{:S(2)}) async-start(f32[128,16,128]{2,1,0:T(8,128)} %bitcast.21), calls=%async_computation.2 | async-start | bytes 2097152 | tf_op jit(solution)/shard_map/all_to_all | solution.py:111
  147.3 5.3 %collective-permute-start.1 = (f32[1,64,128]{2,1,0:T(8,128)S(1)}, f32[1,64,128]{2,1,0:T(8,128)S(1)}, u32[]{:S(2)}, u32[]{:S(2)}) collective-permute-start(f32[1,64,128]{2,1,0:T(8,128)S(1)} %get-tuple-element.70), channel_id=1, source_target_pairs={{0,16},{16,32},{32,48},{48,64},{64,80},{80,96},{96,112},{1,17},{17... | collective-permute-start | bytes 98312 | tf_op jit(solution)/shard_map/ppermute | solution.py:24
  150.7 5.2 %collective-permute-start = (f32[1,64,128]{2,1,0:T(8,128)S(1)}, f32[1,64,128]{2,1,0:T(8,128)S(1)}, u32[]{:S(2)}, u32[]{:S(2)}) collective-permute-start(f32[1,64,128]{2,1,0:T(8,128)S(1)} %get-tuple-element.71), channel_id=1, source_target_pairs={{16,0},{32,16},{48,32},{64,48},{80,64},{96,80},{112,96},{17,1},{33... | collective-permute-start | bytes 98312 | tf_op jit(solution)/shard_map/ppermute | solution.py:26
  156.0 3.8 %collective-permute-start.3 = (f32[66,1,128]{2,1,0:T(1,128)S(1)}, f32[66,1,128]{2,1,0:T(1,128)S(1)}, u32[]{:S(2)}, u32[]{:S(2)}) collective-permute-start(f32[66,1,128]{2,1,0:T(1,128)S(1)} %get-tuple-element.66), channel_id=1, source_target_pairs={{0,1},{1,2},{2,3},{3,4},{4,5},{5,6},{6,7},{7,8},{8,9},{9,10},{10,1... | collective-permute-start | bytes 101384 | tf_op jit(solution)/shard_map/ppermute | solution.py:24
  158.2 4.7 %collective-permute-start.2 = (f32[66,1,128]{2,1,0:T(1,128)S(1)}, f32[66,1,128]{2,1,0:T(1,128)S(1)}, u32[]{:S(2)}, u32[]{:S(2)}) collective-permute-start(f32[66,1,128]{2,1,0:T(1,128)S(1)} %get-tuple-element.67), channel_id=1, source_target_pairs={{1,0},{2,1},{3,2},{4,3},{5,4},{6,5},{7,6},{8,7},{9,8},{10,9},{11,1... | collective-permute-start | bytes 101384 | tf_op jit(solution)/shard_map/ppermute | solution.py:26
  170.7 5.3 %collective-permute-start.5 = (f32[1,64,128]{2,1,0:T(8,128)S(1)}, f32[1,64,128]{2,1,0:T(8,128)S(1)}, u32[]{:S(2)}, u32[]{:S(2)}) collective-permute-start(f32[1,64,128]{2,1,0:T(8,128)S(1)} %get-tuple-element.68), channel_id=1, source_target_pairs={{0,16},{16,32},{32,48},{48,64},{64,80},{80,96},{96,112},{1,17},{17... | collective-permute-start | bytes 98312 | tf_op jit(solution)/shard_map/ppermute | solution.py:24
  174.0 5.2 %collective-permute-start.4 = (f32[1,64,128]{2,1,0:T(8,128)S(1)}, f32[1,64,128]{2,1,0:T(8,128)S(1)}, u32[]{:S(2)}, u32[]{:S(2)}) collective-permute-start(f32[1,64,128]{2,1,0:T(8,128)S(1)} %get-tuple-element.69), channel_id=1, source_target_pairs={{16,0},{32,16},{48,32},{64,48},{80,64},{96,80},{112,96},{17,1},{33... | collective-permute-start | bytes 98312 | tf_op jit(solution)/shard_map/ppermute | solution.py:26
  179.3 3.0 %collective-permute-start.7 = (f32[66,1,128]{2,1,0:T(1,128)S(1)}, f32[66,1,128]{2,1,0:T(1,128)S(1)}, u32[]{:S(2)}, u32[]{:S(2)}) collective-permute-start(f32[66,1,128]{2,1,0:T(1,128)S(1)} %get-tuple-element.64), channel_id=1, source_target_pairs={{0,1},{1,2},{2,3},{3,4},{4,5},{5,6},{6,7},{7,8},{8,9},{9,10},{10,1... | collective-permute-start | bytes 101384 | tf_op jit(solution)/shard_map/ppermute | solution.py:24
  181.0 5.2 %collective-permute-start.6 = (f32[66,1,128]{2,1,0:T(1,128)S(1)}, f32[66,1,128]{2,1,0:T(1,128)S(1)}, u32[]{:S(2)}, u32[]{:S(2)}) collective-permute-start(f32[66,1,128]{2,1,0:T(1,128)S(1)} %get-tuple-element.65), channel_id=1, source_target_pairs={{1,0},{2,1},{3,2},{4,3},{5,4},{6,5},{7,6},{8,7},{9,8},{10,9},{11,1... | collective-permute-start | bytes 101384 | tf_op jit(solution)/shard_map/ppermute | solution.py:26
where the time goes:
time: 199 us; the launch traced here: 195 us
  other arithmetic  67.7 us (34%)
  starting transfers between devices  42.9 us (22%)
  waiting for transfers between devices  36.6 us (18%)
  local copies, waits for them, and re-layouts  29.9 us (15%)
  matrix products  16.7 us (8%)
    reduce_sum x4, other arithmetic, one_block(): jnp.sum(jnp.where(hits, block_margin[:, :, None], jnp.float32(0.0)), axis=0)  44.2 us
    all_to_all x1, waiting for transfers between devices, body(): lax.all_to_all(outgoing.reshape(device_count, capacity, depth), ('brick',...  17.3 us
    dot_general x1, matrix products, body(): jnp.dot(selector, arrived, precision=lax.Precision.HIGHEST, preferred_ele...  16.5 us
    ppermute x4, waiting for transfers between devices, padded(): lax.ppermute(head, axis, [((i + 1) % count, i) for i in range(ends)])  13.6 us
    all_to_all x1, starting transfers between devices, body(): lax.all_to_all(requests, ('brick', 'dom'), split_axis=0, concat_axis=0, t...  11.5 us
    ppermute x4, starting transfers between devices, padded(): lax.ppermute(tail, axis, [(i, (i + 1) % count) for i in range(ends)])  10.6 us
    all_to_all x1, starting transfers between devices, body(): lax.all_to_all(outgoing.reshape(device_count, capacity, depth), ('brick',...  9.82 us
    add x2, other arithmetic, jacobi_extended(): middle + relax * (source - (center * middle - radius_sq * near)) / center  9.27 us
  transfers between devices with their start and end apart: 11, of which 6 were waited for; matrix products, arithmetic and copies ran while one was open for 30% of the time, Pallas kernels for 0%

commit v1 on v0

v1 whole, which is shorter than its diff:
```python
import functools
import math

import jax
import jax.numpy as jnp
from jax import lax
from jax.experimental import pallas as pl
from jax.experimental.pallas import tpu as pltpu
from jax.sharding import PartitionSpec as P

MESH = pl.DeviceIdType.MESH
CAP = 16
LANES = 128
SHARP = 8.0
THRESHOLD = 0.5
T0 = math.tanh(SHARP * THRESHOLD)
RAMP = 0.1
F32 = jnp.float32
BF16 = jnp.bfloat16
YO = 8
NT = (((1,), (1,)), ((), ()))
NN = (((1,), (0,)), ((), ()))


def mm(a, b, dims=NN):
    return lax.dot_general(a, b, dims, preferred_element_type=F32)


def iota(shape, dim):
    return lax.broadcasted_iota(jnp.int32, shape, dim)


def onehot(mask):
    return jnp.where(mask, 1.0, 0.0).astype(F32)


def split2(x):
    hi = x.astype(BF16)
    return hi, (x - hi.astype(F32)).astype(BF16)


def split3(x):
    hi = x.astype(BF16)
    rest = x - hi.astype(F32)
    mid = rest.astype(BF16)
    return hi, mid, (rest - mid.astype(F32)).astype(BF16)


def kernel(
    nb, nd, wx, wy, coup, jac, own, loc, vel_h, adj_h, off_h, mar_h, fil_h,
    res_h, den,
    vel, adj, off, mar, th, mt, pos, wt, msend, mrecv, send, recv, ids_v, ids_s, plane,
    rows, acc, dsend, drecv, ext, fst, out,
    in_sem, smem_sem, msem, mrsem, ssem, rsem, dsem, drsem, hsem, hrsem, osem,
):
    ndev = nb * nd
    count = own.shape[1]
    blocks = count // LANES
    voxel_rows = wx * wy
    slots = ndev * CAP
    gsrc = 16
    grows = gsrc * CAP
    groups = ndev // gsrc
    brick = lax.axis_index("brick")
    dom = lax.axis_index("dom")
    me = brick * nd + dom

    def dev(lin):
        return (lin // nd, lin % nd)

    loads = [
        pltpu.make_async_copy(h, v, in_sem.at[i])
        for i, (h, v) in enumerate(((vel_h, vel), (adj_h, adj), (off_h, off), (mar_h, mar), (fil_h, th)))
    ]
    for load in loads:
        load.start()

    barrier = pltpu.get_barrier_semaphore()

    @pl.loop(1, ndev)
    def _(i):
        pl.semaphore_signal(
            barrier, inc=1, device_id=dev((me + (ndev - i)) % ndev), device_id_type=MESH
        )

    rel = (own[...] - me + ndev) % ndev
    rr = iota((LANES, 2 * LANES), 0)
    cc = iota((LANES, 2 * LANES), 1)
    upper = onehot((rr < cc) | (cc >= LANES)).astype(BF16)
    base = jnp.zeros((ndev, LANES), F32)
    for b in range(blocks):
        sl = slice(b * LANES, (b + 1) * LANES)
        hit = onehot(rel[:, sl] == iota((ndev, LANES), 0))
        hitb = hit.astype(BF16)
        mt[:, sl] = hitb
        counted = mm(hitb, upper)
        pos[:, sl] = jnp.sum((counted[:, :LANES] + base) * hit, axis=0, keepdims=True)
        base = base + counted[:, LANES:]
    posi = pos[...].astype(jnp.int32)
    placed = rel * CAP + posi

    loads[0].wait()
    loads[1].wait()
    total = None
    for c in range(3):
        part = vel[c].astype(F32) * mm(coup[...], adj[c])
        total = part if total is None else total + part
    product = jac[...] * jnp.sum(total, axis=0, keepdims=True)

    kmask = (iota((LANES, count), 0) % CAP) == posi
    ids = loc[...]

    def rows_of(value):
        return mm(mt[...], jnp.where(kmask, value, 0.0).astype(BF16), NT)

    id_rows = 64.0 * rows_of((ids // 64).astype(F32)) + rows_of((ids % 64).astype(F32))
    p1, p2, p3 = split3(product)
    p_rows = rows_of(p1.astype(F32)) + (rows_of(p2.astype(F32)) + rows_of(p3.astype(F32)))
    jrow = iota((ndev, LANES), 0) % 8
    jlane = iota((ndev, LANES), 1) // CAP
    is_id = jlane == jrow
    is_p = jlane == (jrow + 4) % 8
    msend[...] = jnp.where(is_id, id_rows, jnp.where(is_p, p_rows, 0.0))

    loads[2].wait()
    loads[3].wait()
    vrow = iota((LANES, LANES), 0)
    for b in range(blocks):
        sl = slice(b * LANES, (b + 1) * LANES)

        def slot8(i, total):
            at = pl.ds(pl.multiple_of(i * 8, 8), 8)
            o8 = off[at, sl]
            m8 = mar[at, sl]
            for k in range(8):
                total = total + jnp.where(o8[k : k + 1] == vrow, m8[k : k + 1], 0.0)
            return total

        built = lax.fori_loop(0, off.shape[0] // 8, slot8, jnp.zeros((LANES, LANES), F32))
        hi, lo = split2(built)
        wt[0:LANES, sl] = hi
        wt[LANES : 2 * LANES, sl] = lo

    pl.semaphore_wait(barrier, ndev - 1)

    def row_copy(src, dst, send_sem, recv_sem, lin):
        return pltpu.make_async_remote_copy(
            src_ref=src, dst_ref=dst, send_sem=send_sem, recv_sem=recv_sem,
            device_id=dev(lin), device_id_type=MESH,
        )

    pltpu.make_async_copy(msend.at[pl.ds(0, 1)], mrecv.at[pl.ds(0, 1)], mrsem).start()

    @pl.loop(1, ndev)
    def _(i):
        j = ndev - i
        row = pl.ds(j, 1)
        row_copy(msend.at[row], mrecv.at[row], msem, mrsem, (me + j) % ndev).start()

    @pl.loop(0, groups)
    def _(i):
        g = groups - 1 - i
        start = pl.multiple_of(g * grows, grows)
        pick = onehot(placed == iota((grows, count), 0) + start).astype(BF16)
        both = mm(pick, wt[...], NT)
        send[pl.ds(start, grows), :] = both[:, :LANES] + both[:, LANES:]

        @pl.loop(0, gsrc)
        def _(q):
            j = g * gsrc + (gsrc - 1 - q)
            at = pl.ds(pl.multiple_of(j * CAP, CAP), CAP)

            @pl.when(j > 0)
            def _():
                row_copy(send.at[at], recv.at[at], ssem, rsem.at[g], (me + j) % ndev).start()

            @pl.when(j == 0)
            def _():
                pltpu.make_async_copy(send.at[at], recv.at[at], rsem.at[g]).start()

    loads[4].wait()

    @pl.loop(0, wx)
    def _(x):
        at = pl.ds(pl.multiple_of(x * wy, wy), wy)
        th[at, :] = jnp.tanh(SHARP * (th[at, :] - THRESHOLD))
        acc[at, :] = jnp.zeros((wy, LANES), F32)

    pltpu.make_async_copy(mrecv, mrecv, mrsem).wait()
    got = mrecv[...]
    chunk_ids = jnp.sum(jnp.where(is_id, got, 0.0).reshape(ndev // 8, 8, LANES), axis=1)
    chunk_p = jnp.sum(jnp.where(is_p, got, 0.0).reshape(ndev // 8, 8, LANES), axis=1)
    plane[...] = pltpu.roll(chunk_p, LANES // 2, axis=1)
    ids_v[...] = chunk_ids.astype(jnp.int32)
    to_smem = pltpu.make_async_copy(ids_v, ids_s, smem_sem)
    to_smem.start()
    to_smem.wait()

    @pl.loop(0, slots // 8)
    def _(r8):
        c = r8 // 16
        l0 = (r8 % 16) * 8
        for k in range(8):
            at = jnp.minimum(jnp.maximum(ids_s[c, l0 + k], 0), voxel_rows - 1)
            rows[pl.ds(pl.multiple_of(r8 * 8, 8) + k, 1), :] = th[pl.ds(at, 1), :]

    eye = iota((LANES, LANES), 0) == iota((LANES, LANES), 1)
    yrow = iota((wy, grows), 0)
    per = 8

    @pl.loop(0, groups)
    def _(i):
        g = groups - 1 - i
        at = pl.ds(pl.multiple_of(g * grows, grows), grows)
        pltpu.make_async_copy(recv.at[at], recv.at[at], rsem.at[g]).wait()
        w = recv[at, :]
        d = jnp.sum((rows[at, :] + T0) * w, axis=1, keepdims=True) * (1.0 / (2.0 * T0))
        halves = grows // LANES
        pcol = []
        idrow = []
        for h in range(halves):
            c = g * halves + h
            dcol = d[h * LANES : (h + 1) * LANES]
            dsend[pl.ds(c, 1), :] = jnp.sum(jnp.where(eye, dcol, 0.0), axis=0, keepdims=True)
            pcol.append(jnp.sum(jnp.where(eye, plane[pl.ds(c, 1), :], 0.0), axis=1, keepdims=True))
            idrow.append(ids_v[pl.ds(c, 1), :])
        p = jnp.concatenate(pcol, axis=0)
        near = RAMP + d
        term = -RAMP * (1.0 + RAMP) / (near * near) * p
        hi, lo = split2(term * w)
        both = jnp.concatenate([hi, lo], axis=1)
        idr = jnp.concatenate(idrow, axis=1)
        xid = idr // wy
        yhot = onehot(yrow == idr % wy)

        @pl.loop(0, gsrc)
        def _(q):
            j = g * gsrc + q
            c = j // 8

            @pl.when(j > 0)
            def _():
                row_copy(
                    dsend.at[pl.ds(c, 1)], drecv.at[pl.ds(j, 1)], dsem, drsem, (me + (ndev - j)) % ndev
                ).start()

            @pl.when(j == 0)
            def _():
                pltpu.make_async_copy(dsend.at[pl.ds(c, 1)], drecv.at[pl.ds(j, 1)], drsem).start()

        @pl.loop(0, wx // per)
        def _(xb):
            pick = jnp.concatenate(
                [jnp.where(xid == xb * per + u, yhot, 0.0) for u in range(per)], axis=0
            ).astype(BF16)
            added = mm(pick, both)
            xs = pl.ds(pl.multiple_of(xb * per * wy, per * wy), per * wy)
            acc[xs, :] = acc[xs, :] + (added[:, :LANES] + added[:, LANES:])

    @pl.loop(0, wx)
    def _(x):
        at = pl.ds(pl.multiple_of(x * wy, wy), wy)
        t = th[at, :]
        ext[x + 2, YO : YO + wy, :] = acc[at, :] * ((SHARP / (2.0 * T0)) * (1.0 - t * t))

    xl, xh = (brick + (nb - 1)) % nb, (brick + 1) % nb
    yl, yh = (dom + (nd - 1)) % nd, (dom + 1) % nd
    ys, y_all = pl.ds(YO, wy), pl.ds(2, wx)
    moves = [
        ((pl.ds(2, 2), ys), (pl.ds(wx + 2, 2), ys), (xl, dom)),
        ((pl.ds(wx, 2), ys), (pl.ds(0, 2), ys), (xh, dom)),
        ((y_all, pl.ds(YO, 2)), (y_all, pl.ds(YO + wy, 2)), (brick, yl)),
        ((y_all, pl.ds(YO + wy - 2, 2)), (y_all, pl.ds(YO - 2, 2)), (brick, yh)),
        ((pl.ds(2, 1), pl.ds(YO, 1)), (pl.ds(wx + 2, 1), pl.ds(YO + wy, 1)), (xl, yl)),
        ((pl.ds(2, 1), pl.ds(YO + wy - 1, 1)), (pl.ds(wx + 2, 1), pl.ds(YO - 1, 1)), (xl, yh)),
        ((pl.ds(wx + 1, 1), pl.ds(YO, 1)), (pl.ds(1, 1), pl.ds(YO + wy, 1)), (xh, yl)),
        ((pl.ds(wx + 1, 1), pl.ds(YO + wy - 1, 1)), (pl.ds(1, 1), pl.ds(YO - 1, 1)), (xh, yh)),
    ]
    halos = [
        pltpu.make_async_remote_copy(
            src_ref=ext.at[s], dst_ref=ext.at[t], send_sem=hsem.at[i], recv_sem=hrsem.at[i],
            device_id=to, device_id_type=MESH,
        )
        for i, (s, t, to) in enumerate(moves)
    ]
    for halo in halos:
        halo.start()
    for halo in halos:
        halo.wait()

    wide = ext.shape[1]
    yline = iota((wide, LANES), 0)
    zline = iota((wide, LANES), 1)
    first_y = jnp.where(dom == 0, YO, 0)
    last_y = jnp.where(dom == nd - 1, YO + wy, wide)
    inside = (yline >= first_y) & (yline < last_y)

    for edge, first_x in ((brick == 0, 0), (brick == nb - 1, wx + 2)):

        @pl.when(edge)
        def _():
            ext[first_x : first_x + 2] = jnp.zeros((2, wide, LANES), F32)

    def around(ref, x):
        y = ref[x]
        total = ref[x + 1] + ref[x - 1]
        total = total + pltpu.roll(y, 1, axis=0) + pltpu.roll(y, wide - 1, axis=0)
        total = total + jnp.where(zline == 0, 0.0, pltpu.roll(y, 1, axis=1))
        total = total + jnp.where(zline == LANES - 1, 0.0, pltpu.roll(y, LANES - 1, axis=1))
        return y, total

    @pl.loop(0, wx + 4)
    def _(x):
        ext[x] = jnp.where(inside, ext[x], 0.0)

    @pl.loop(0, wx + 2)
    def _(x):
        y, near = around(ext, x + 1)
        fst[x + 1] = jnp.where(inside, 0.19 * y + 0.135 * near, 0.0)

    for edge, first_x in ((brick == 0, 1), (brick == nb - 1, wx + 2)):

        @pl.when(edge)
        def _():
            fst[first_x] = jnp.zeros((wide, LANES), F32)

    @pl.loop(0, wx)
    def _(x):
        y, near = around(fst, x + 2)
        new = 0.1 * y + 0.09 * ext[x + 2] + 0.135 * near
        out[x] = new[YO : YO + wy]

    store = pltpu.make_async_copy(out, res_h, osem)
    store.start()

    pltpu.make_async_copy(drecv, drecv, drsem).wait()
    back = jnp.where(is_id, drecv[...], 0.0).T
    spread = None
    for piece in split3(back):
        part = mm(piece, mt[...])
        spread = part if spread is None else spread + part
    den[...] = jnp.sum(jnp.where(kmask, spread, 0.0), axis=0, keepdims=True)

    others = pl.ds(1, ndev - 1)
    row_copy(msend.at[others], mrecv.at[others], msem, mrsem, me).wait_send()
    most = pl.ds(CAP, slots - CAP)
    row_copy(send.at[most], recv.at[most], ssem, rsem.at[0], me).wait_send()
    row_copy(drecv.at[others], drecv.at[others], dsem, drsem, me).wait_send()
    store.wait()


def body(velocity, adjoint, coupling, jac_weight, owner, local_block, offsets, margin, filtered):
    nb, nd = lax.axis_size("brick"), lax.axis_size("dom")
    ndev = nb * nd
    count = owner.shape[0]
    wx, wy, depth = filtered.shape
    slots = ndev * CAP
    wide = wy + 16
    vmem = pl.BlockSpec(memory_space=pltpu.VMEM)
    hbm = pl.BlockSpec(memory_space=pl.ANY)
    dma = pltpu.SemaphoreType.DMA
    result, density = pl.pallas_call(
        functools.partial(kernel, nb, nd, wx, wy),
        out_shape=(
            jax.ShapeDtypeStruct(filtered.shape, F32),
            jax.ShapeDtypeStruct((1, count), F32),
        ),
        in_specs=[vmem] * 4 + [hbm] * 5,
        out_specs=(hbm, vmem),
        scratch_shapes=[
            pltpu.VMEM(velocity.shape, BF16),
            pltpu.VMEM(adjoint.shape, BF16),
            pltpu.VMEM(offsets.shape, jnp.int32),
            pltpu.VMEM(margin.shape, F32),
            pltpu.VMEM((wx * wy, LANES), F32),
            pltpu.VMEM((ndev, count), BF16),
            pltpu.VMEM((1, count), F32),
            pltpu.VMEM((2 * LANES, count), BF16),
            pltpu.VMEM((ndev, LANES), F32),
            pltpu.VMEM((ndev, LANES), F32),
            pltpu.VMEM((slots, LANES), F32),
            pltpu.VMEM((slots, LANES), F32),
            pltpu.VMEM((ndev // 8, LANES), jnp.int32),
            pltpu.SMEM((ndev // 8, LANES), jnp.int32),
            pltpu.VMEM((ndev // 8, LANES), F32),
            pltpu.VMEM((slots, LANES), F32),
            pltpu.VMEM((wx * wy, LANES), F32),
            pltpu.VMEM((ndev // 8, LANES), F32),
            pltpu.VMEM((ndev, LANES), F32),
            pltpu.VMEM((wx + 4, wide, LANES), F32),
            pltpu.VMEM((wx + 4, wide, LANES), F32),
            pltpu.VMEM(filtered.shape, F32),
            dma((5,)), dma, dma, dma, dma, dma((ndev // 16,)), dma, dma, dma((8,)), dma((8,)), dma,
        ],
        compiler_params=pltpu.CompilerParams(
            collective_id=0, has_side_effects=True, vmem_limit_bytes=60 * 1024 * 1024
        ),
        name="sensitivity",
    )(
        coupling, jac_weight.reshape(1, count), owner.reshape(1, count),
        local_block.reshape(1, count), velocity, adjoint, offsets, margin,
        filtered.reshape(wx * wy, depth),
    )
    return result, density.reshape(count)


def solution(mesh):
    return jax.shard_map(
        body,
        mesh=mesh,
        in_specs=(
            P(None, None, ("brick", "dom")),
            P(None, None, ("brick", "dom")),
            P(),
            P(("brick", "dom")),
            P(("brick", "dom"), None),
            P(("brick", "dom")),
            P(None, ("brick", "dom")),
            P(None, ("brick", "dom")),
            P("brick", "dom", None),
        ),
        out_specs=(P("brick", "dom", None), P(("brick", "dom"))),
        check_vma=False,
    )
```

time: 199 us -> 85.1 us (0.43); the launches traced: 195 us -> 84.9 us
  Pallas kernels: 0 us -> 80.5 us
  other arithmetic: 67.7 us -> 0 us
  starting transfers between devices: 42.9 us -> 0 us
  waiting for transfers between devices: 36.6 us -> 0 us
  local copies, waits for them, and re-layouts: 29.9 us -> 3.76 us
  matrix products: 16.7 us -> 0 us
    pallas_call x0 -> x1, Pallas kernels: none -> 80.5 us  [body(): pl.pallas_call(functools.partial(kernel, nb, nd, wx, wy), out_shape=(jax....]
    reduce_sum x6 -> x0, other arithmetic: 44.8 us -> none  [the longest x4 44.2 us: one_block(): jnp.sum(jnp.where(hits, block_margin[:, :, None], jnp.float32(0.0)), axis=0)]
    all_to_all x3 -> x0, starting transfers between devices: 25.6 us -> none  [the longest x1 11.5 us: body(): lax.all_to_all(requests, ('brick', 'dom'), split_axis=0, concat_axis=0, t...]
    all_to_all x3 -> x0, waiting for transfers between devices: 23 us -> none  [the longest x1 17.3 us: body(): lax.all_to_all(outgoing.reshape(device_count, capacity, depth), ('brick',...]
    ppermute x8 -> x0, starting transfers between devices: 17.3 us -> none  [the longest x4 10.6 us: padded(): lax.ppermute(tail, axis, [(i, (i + 1) % count) for i in range(ends)])]
    dot_general x2 -> x0, matrix products: 16.7 us -> none  [the longest x1 16.5 us: body(): jnp.dot(selector, arrived, precision=lax.Precision.HIGHEST, preferred_ele...]
    ppermute x8 -> x0, waiting for transfers between devices: 13.6 us -> none  [the longest x4 13.6 us: padded(): lax.ppermute(head, axis, [((i + 1) % count, i) for i in range(ends)])]
    add x2 -> x0, other arithmetic: 9.27 us -> none  [jacobi_extended(): middle + relax * (source - (center * middle - radius_sq * near)) / center]
  transfers between devices with their start and end apart: 11 -> 0, of which waited for: 6 -> 0; matrix products, arithmetic and copies ran while one was open for 30% -> 0% of each run, Pallas kernels for 0% -> 0%
where the time goes in v1:
time: 85.1 us; the launch traced here: 84.9 us
  Pallas kernels  80.5 us (95%)
  local copies, waits for them, and re-layouts  3.76 us (4%)
    pallas_call x1, Pallas kernels, body(): pl.pallas_call(functools.partial(kernel, nb, nd, wx, wy), out_shape=(jax....  80.5 us
    unnamed x4, local copies, waits for them, and re-layouts  3.76 us

profile of v1, /device:TPU:1, one launch (start us, length us, event | category | flops | bytes accessed | tf_op | source)
XLA Modules:
  0.0 84.9 jit_solution(11505291385594993784)
XLA Ops:
  0.6 80.5 %sensitivity.1 = (f32[64,64,128]{2,1,0:T(8,128)}, f32[1,1024]{1,0:T(1,128)}) custom-call(bf16[27,27]{1,0:T(8,128)(2,1)} %coup.1, f32[1,1024]{1,0:T(1,128)} %bitcast.7, s32[1,1024]{1,0:T(1,128)} %bitcast.8, s32[1,1024]{1,0:T(1,128)} %bitcast.9, bf16[3,27,1024]{2,1,0:T(8,128)(2,1)} %vel_h.1, bf16[3,27,1024]{2,1,0:T(8,128)(2,1)} %adj_h.1, s32[128,1024]{1,0:T(8,128)} %off_h.1, ...), custom_call_target="tpu_custom_call" | custom-call | tf_op jit(solution)/shard_map/sensitivity/pallas_call | solution.py:362
  81.1 0.0 copy-start
  81.1 3.2 %copy.13 = f32[64,64,128]{2,1,0:T(8,128)} copy(f32[64,64,128]{2,1,0:T(8,128)} %get-tuple-element.8) | data formatting | bytes 4194304
  84.3 0.0 copy-done
  84.3 0.6 copy.14
Async XLA Ops:
  81.1 3.2 %copy-start = (f32[1,1024]{1,0:T(1,128)S(1)}, f32[1,1024]{1,0:T(1,128)}, u32[]{:S(2)}) copy-start(f32[1,1024]{1,0:T(1,128)} %get-tuple-element.5) | copy-start | bytes 12292

commit v2 on v1

--- a/solution.py
+++ b/solution.py
@@ -49,7 +49,7 @@
 def kernel(
     nb, nd, wx, wy, coup, jac, own, loc, vel_h, adj_h, off_h, mar_h, fil_h,
     res_h, den,
-    vel, adj, off, mar, th, mt, pos, wt, msend, mrecv, send, recv, ids_v, ids_s, plane,
+    vel, adj, off, mar, th, mt, pos, wt, fine, parts, msend, mrecv, send, recv, ids_v, ids_s, pcol,
     rows, acc, dsend, drecv, ext, fst, out,
     in_sem, smem_sem, msem, mrsem, ssem, rsem, dsem, drsem, hsem, hrsem, osem,
 ):
@@ -87,15 +87,15 @@
     rr = iota((LANES, 2 * LANES), 0)
     cc = iota((LANES, 2 * LANES), 1)
     upper = onehot((rr < cc) | (cc >= LANES)).astype(BF16)
+    hits = [onehot(rel[:, b * LANES : (b + 1) * LANES] == iota((ndev, LANES), 0)) for b in range(blocks)]
+    counted = mm(jnp.concatenate(hits, axis=0).astype(BF16), upper)
     base = jnp.zeros((ndev, LANES), F32)
     for b in range(blocks):
         sl = slice(b * LANES, (b + 1) * LANES)
-        hit = onehot(rel[:, sl] == iota((ndev, LANES), 0))
-        hitb = hit.astype(BF16)
-        mt[:, sl] = hitb
-        counted = mm(hitb, upper)
-        pos[:, sl] = jnp.sum((counted[:, :LANES] + base) * hit, axis=0, keepdims=True)
-        base = base + counted[:, LANES:]
+        here = counted[b * ndev : (b + 1) * ndev]
+        mt[:, sl] = hits[b].astype(BF16)
+        pos[:, sl] = jnp.sum((here[:, :LANES] + base) * hits[b], axis=0, keepdims=True)
+        base = base + here[:, LANES:]
     posi = pos[...].astype(jnp.int32)
     placed = rel * CAP + posi
 
@@ -107,15 +107,15 @@
         total = part if total is None else total + part
     product = jac[...] * jnp.sum(total, axis=0, keepdims=True)
 
-    kmask = (iota((LANES, count), 0) % CAP) == posi
+    kmask = iota((CAP, count), 0) == posi
     ids = loc[...]
-
-    def rows_of(value):
-        return mm(mt[...], jnp.where(kmask, value, 0.0).astype(BF16), NT)
-
-    id_rows = 64.0 * rows_of((ids // 64).astype(F32)) + rows_of((ids % 64).astype(F32))
-    p1, p2, p3 = split3(product)
-    p_rows = rows_of(p1.astype(F32)) + (rows_of(p2.astype(F32)) + rows_of(p3.astype(F32)))
+    values = [(ids // 64).astype(F32), (ids % 64).astype(F32)]
+    values += [piece.astype(F32) for piece in split3(product)]
+    stack = jnp.concatenate([jnp.where(kmask, v, 0.0) for v in values], axis=0).astype(BF16)
+    lined = mm(stack, mt[...], NT)
+    pieces = [lined[u * CAP : (u + 1) * CAP] for u in range(5)]
+    id_rows = jnp.concatenate([64.0 * pieces[0] + pieces[1]] * 8, axis=0).T
+    p_rows = jnp.concatenate([pieces[2] + (pieces[3] + pieces[4])] * 8, axis=0).T
     jrow = iota((ndev, LANES), 0) % 8
     jlane = iota((ndev, LANES), 1) // CAP
     is_id = jlane == jrow
@@ -124,22 +124,54 @@
 
     loads[2].wait()
     loads[3].wait()
-    vrow = iota((LANES, LANES), 0)
+    entries = off.shape[0]
+    tiles = LANES // 8
+    sub = iota((8, LANES), 0)
     for b in range(blocks):
         sl = slice(b * LANES, (b + 1) * LANES)
 
-        def slot8(i, total):
+        @pl.loop(0, entries // 8)
+        def _(i):
             at = pl.ds(pl.multiple_of(i * 8, 8), 8)
             o8 = off[at, sl]
             m8 = mar[at, sl]
+            fine[at, :] = o8 % 8
+            tile = o8 // 8
+            for u in range(tiles):
+                parts[u, at, :] = jnp.where(tile == u, m8, 0.0)
+
+        def slot8(i, totals):
+            totals = list(totals)
             for k in range(8):
-                total = total + jnp.where(o8[k : k + 1] == vrow, m8[k : k + 1], 0.0)
-            return total
-
-        built = lax.fori_loop(0, off.shape[0] // 8, slot8, jnp.zeros((LANES, LANES), F32))
+                row = pl.ds(i * 8 + k, 1)
+                hit = jnp.broadcast_to(fine[row, :], (8, LANES)) == sub
+                for u in range(tiles):
+                    part = jnp.broadcast_to(parts[u, row, :], (8, LANES))
+                    totals[u] = totals[u] + jnp.where(hit, part, 0.0)
+            return tuple(totals)
+
+        zero = jnp.zeros((8, LANES), F32)
+        built = jnp.concatenate(lax.fori_loop(0, entries // 8, slot8, (zero,) * tiles), axis=0)
         hi, lo = split2(built)
         wt[0:LANES, sl] = hi
         wt[LANES : 2 * LANES, sl] = lo
+
+    prows = min(slots, 512)
+
+    @pl.loop(0, slots // prows)
+    def _(g):
+        start = pl.multiple_of(g * prows, prows)
+        pick = onehot(placed == iota((prows, count), 0) + start).astype(BF16)
+        both = mm(pick, wt[...], NT)
+        send[pl.ds(start, prows), :] = both[:, :LANES] + both[:, LANES:]
+
+    loads[4].wait()
+
+    @pl.loop(0, wx)
+    def _(x):
+        at = pl.ds(pl.multiple_of(x * wy, wy), wy)
+        th[at, :] = jnp.tanh(SHARP * (th[at, :] - THRESHOLD))
+        acc[at, :] = jnp.zeros((wy, LANES), F32)
 
     pl.semaphore_wait(barrier, ndev - 1)
 
@@ -157,44 +189,29 @@
         row = pl.ds(j, 1)
         row_copy(msend.at[row], mrecv.at[row], msem, mrsem, (me + j) % ndev).start()
 
-    @pl.loop(0, groups)
+    own_rows = pl.ds(0, CAP)
+    pltpu.make_async_copy(send.at[own_rows], recv.at[own_rows], rsem.at[0]).start()
+
+    @pl.loop(1, ndev)
     def _(i):
-        g = groups - 1 - i
-        start = pl.multiple_of(g * grows, grows)
-        pick = onehot(placed == iota((grows, count), 0) + start).astype(BF16)
-        both = mm(pick, wt[...], NT)
-        send[pl.ds(start, grows), :] = both[:, :LANES] + both[:, LANES:]
-
-        @pl.loop(0, gsrc)
-        def _(q):
-            j = g * gsrc + (gsrc - 1 - q)
-            at = pl.ds(pl.multiple_of(j * CAP, CAP), CAP)
-
-            @pl.when(j > 0)
-            def _():
-                row_copy(send.at[at], recv.at[at], ssem, rsem.at[g], (me + j) % ndev).start()
-
-            @pl.when(j == 0)
-            def _():
-                pltpu.make_async_copy(send.at[at], recv.at[at], rsem.at[g]).start()
-
-    loads[4].wait()
-
-    @pl.loop(0, wx)
-    def _(x):
-        at = pl.ds(pl.multiple_of(x * wy, wy), wy)
-        th[at, :] = jnp.tanh(SHARP * (th[at, :] - THRESHOLD))
-        acc[at, :] = jnp.zeros((wy, LANES), F32)
+        j = ndev - i
+        at = pl.ds(pl.multiple_of(j * CAP, CAP), CAP)
+        row_copy(send.at[at], recv.at[at], ssem, rsem.at[j // gsrc], (me + j) % ndev).start()
 
     pltpu.make_async_copy(mrecv, mrecv, mrsem).wait()
     got = mrecv[...]
     chunk_ids = jnp.sum(jnp.where(is_id, got, 0.0).reshape(ndev // 8, 8, LANES), axis=1)
     chunk_p = jnp.sum(jnp.where(is_p, got, 0.0).reshape(ndev // 8, 8, LANES), axis=1)
-    plane[...] = pltpu.roll(chunk_p, LANES // 2, axis=1)
+    p_lines = pltpu.roll(chunk_p, LANES // 2, axis=1)
     ids_v[...] = chunk_ids.astype(jnp.int32)
     to_smem = pltpu.make_async_copy(ids_v, ids_s, smem_sem)
     to_smem.start()
     to_smem.wait()
+
+    eye = iota((LANES, LANES), 0) == iota((LANES, LANES), 1)
+    for c in range(ndev // 8):
+        line = jnp.sum(jnp.where(eye, p_lines[c : c + 1], 0.0), axis=1, keepdims=True)
+        pcol[c * LANES : (c + 1) * LANES, :] = jnp.broadcast_to(line, (LANES, LANES))
 
     @pl.loop(0, slots // 8)
     def _(r8):
@@ -204,9 +221,7 @@
             at = jnp.minimum(jnp.maximum(ids_s[c, l0 + k], 0), voxel_rows - 1)
             rows[pl.ds(pl.multiple_of(r8 * 8, 8) + k, 1), :] = th[pl.ds(at, 1), :]
 
-    eye = iota((LANES, LANES), 0) == iota((LANES, LANES), 1)
     yrow = iota((wy, grows), 0)
-    per = 8
 
     @pl.loop(0, groups)
     def _(i):
@@ -216,17 +231,14 @@
         w = recv[at, :]
         d = jnp.sum((rows[at, :] + T0) * w, axis=1, keepdims=True) * (1.0 / (2.0 * T0))
         halves = grows // LANES
-        pcol = []
         idrow = []
         for h in range(halves):
             c = g * halves + h
             dcol = d[h * LANES : (h + 1) * LANES]
             dsend[pl.ds(c, 1), :] = jnp.sum(jnp.where(eye, dcol, 0.0), axis=0, keepdims=True)
-            pcol.append(jnp.sum(jnp.where(eye, plane[pl.ds(c, 1), :], 0.0), axis=1, keepdims=True))
             idrow.append(ids_v[pl.ds(c, 1), :])
-        p = jnp.concatenate(pcol, axis=0)
         near = RAMP + d
-        term = -RAMP * (1.0 + RAMP) / (near * near) * p
+        term = -RAMP * (1.0 + RAMP) / (near * near) * pcol[at, :]
         hi, lo = split2(term * w)
         both = jnp.concatenate([hi, lo], axis=1)
         idr = jnp.concatenate(idrow, axis=1)
@@ -248,14 +260,9 @@
             def _():
                 pltpu.make_async_copy(dsend.at[pl.ds(c, 1)], drecv.at[pl.ds(j, 1)], drsem).start()
 
-        @pl.loop(0, wx // per)
-        def _(xb):
-            pick = jnp.concatenate(
-                [jnp.where(xid == xb * per + u, yhot, 0.0) for u in range(per)], axis=0
-            ).astype(BF16)
-            added = mm(pick, both)
-            xs = pl.ds(pl.multiple_of(xb * per * wy, per * wy), per * wy)
-            acc[xs, :] = acc[xs, :] + (added[:, :LANES] + added[:, LANES:])
+        pick = jnp.concatenate([jnp.where(xid == x, yhot, 0.0) for x in range(wx)], axis=0)
+        added = mm(pick.astype(BF16), both)
+        acc[...] = acc[...] + (added[:, :LANES] + added[:, LANES:])
 
     @pl.loop(0, wx)
     def _(x):
@@ -288,57 +295,62 @@
     for halo in halos:
         halo.wait()
 
-    wide = ext.shape[1]
-    yline = iota((wide, LANES), 0)
-    zline = iota((wide, LANES), 1)
-    first_y = jnp.where(dom == 0, YO, 0)
-    last_y = jnp.where(dom == nd - 1, YO + wy, wide)
-    inside = (yline >= first_y) & (yline < last_y)
-
     for edge, first_x in ((brick == 0, 0), (brick == nb - 1, wx + 2)):
 
         @pl.when(edge)
         def _():
-            ext[first_x : first_x + 2] = jnp.zeros((2, wide, LANES), F32)
-
-    def around(ref, x):
-        y = ref[x]
-        total = ref[x + 1] + ref[x - 1]
-        total = total + pltpu.roll(y, 1, axis=0) + pltpu.roll(y, wide - 1, axis=0)
+            ext[first_x : first_x + 2] = jnp.zeros((2, ext.shape[1], LANES), F32)
+
+    for edge, first_y in ((dom == 0, YO - 2), (dom == nd - 1, YO + wy)):
+
+        @pl.when(edge)
+        def _():
+            @pl.loop(0, wx + 4)
+            def _(x):
+                ext[x, first_y : first_y + 2, :] = jnp.zeros((2, LANES), F32)
+
+    tall = fst.shape[1]
+
+    def around(ref, x, y0, size):
+        y = ref[x, y0 : y0 + size, :]
+        zline = iota((size, LANES), 1)
+        total = ref[x + 1, y0 : y0 + size, :] + ref[x - 1, y0 : y0 + size, :]
+        total = total + ref[x, y0 + 1 : y0 + 1 + size, :] + ref[x, y0 - 1 : y0 - 1 + size, :]
         total = total + jnp.where(zline == 0, 0.0, pltpu.roll(y, 1, axis=1))
         total = total + jnp.where(zline == LANES - 1, 0.0, pltpu.roll(y, LANES - 1, axis=1))
         return y, total
 
-    @pl.loop(0, wx + 4)
-    def _(x):
-        ext[x] = jnp.where(inside, ext[x], 0.0)
-
-    @pl.loop(0, wx + 2)
-    def _(x):
-        y, near = around(ext, x + 1)
-        fst[x + 1] = jnp.where(inside, 0.19 * y + 0.135 * near, 0.0)
+    line = iota((tall, LANES), 0)
+    inside = (line >= jnp.where(dom == 0, 1, 0)) & (line <= jnp.where(dom == nd - 1, wy, wy + 1))
+
+    @pl.loop(0, (wx + 2) // 2)
+    def _(half):
+        for u in range(2):
+            x = half * 2 + u + 1
+            y, near = around(ext, x, YO - 1, tall)
+            fst[x] = jnp.where(inside, 0.19 * y + 0.135 * near, 0.0)
 
     for edge, first_x in ((brick == 0, 1), (brick == nb - 1, wx + 2)):
 
         @pl.when(edge)
         def _():
-            fst[first_x] = jnp.zeros((wide, LANES), F32)
-
-    @pl.loop(0, wx)
-    def _(x):
-        y, near = around(fst, x + 2)
-        new = 0.1 * y + 0.09 * ext[x + 2] + 0.135 * near
-        out[x] = new[YO : YO + wy]
+            fst[first_x] = jnp.zeros((tall, LANES), F32)
+
+    @pl.loop(0, wx // 2)
+    def _(half):
+        for u in range(2):
+            x = half * 2 + u
+            y, near = around(fst, x + 2, 1, wy)
+            out[x] = 0.1 * y + 0.09 * ext[x + 2, YO : YO + wy, :] + 0.135 * near
 
     store = pltpu.make_async_copy(out, res_h, osem)
     store.start()
 
     pltpu.make_async_copy(drecv, drecv, drsem).wait()
     back = jnp.where(is_id, drecv[...], 0.0).T
-    spread = None
-    for piece in split3(back):
-        part = mm(piece, mt[...])
-        spread = part if spread is None else spread + part
+    packed = jnp.sum(back.reshape(LANES // CAP, CAP, ndev), axis=0)
+    spread = mm(jnp.concatenate([piece for piece in split3(packed)], axis=0), mt[...])
+    spread = spread[:CAP] + (spread[CAP : 2 * CAP] + spread[2 * CAP :])
     den[...] = jnp.sum(jnp.where(kmask, spread, 0.0), axis=0, keepdims=True)
 
     others = pl.ds(1, ndev - 1)
@@ -376,19 +388,21 @@
             pltpu.VMEM((ndev, count), BF16),
             pltpu.VMEM((1, count), F32),
             pltpu.VMEM((2 * LANES, count), BF16),
+            pltpu.VMEM((offsets.shape[0], LANES), jnp.int32),
+            pltpu.VMEM((LANES // 8, offsets.shape[0], LANES), F32),
             pltpu.VMEM((ndev, LANES), F32),
             pltpu.VMEM((ndev, LANES), F32),
             pltpu.VMEM((slots, LANES), F32),
             pltpu.VMEM((slots, LANES), F32),
             pltpu.VMEM((ndev // 8, LANES), jnp.int32),
             pltpu.SMEM((ndev // 8, LANES), jnp.int32),
-            pltpu.VMEM((ndev // 8, LANES), F32),
+            pltpu.VMEM((slots, LANES), F32),
             pltpu.VMEM((slots, LANES), F32),
             pltpu.VMEM((wx * wy, LANES), F32),
             pltpu.VMEM((ndev // 8, LANES), F32),
             pltpu.VMEM((ndev, LANES), F32),
             pltpu.VMEM((wx + 4, wide, LANES), F32),
-            pltpu.VMEM((wx + 4, wide, LANES), F32),
+            pltpu.VMEM((wx + 4, wy + 8, LANES), F32),
             pltpu.VMEM(filtered.shape, F32),
             dma((5,)), dma, dma, dma, dma, dma((ndev // 16,)), dma, dma, dma((8,)), dma((8,)), dma,
         ],

time: 85.1 us -> 69.5 us (0.82)
  Pallas kernels: 80.5 us -> 64.9 us
    pallas_call x1, Pallas kernels: 80.5 us -> 64.9 us  [body(): pl.pallas_call(functools.partial(kernel, nb, nd, wx, wy), out_shape=(jax....]
where the time goes in v2:
time: 69.5 us; the launch traced here: 69.3 us
  Pallas kernels  64.9 us (93%)
  local copies, waits for them, and re-layouts  3.76 us (5%)
    pallas_call x1, Pallas kernels, body(): pl.pallas_call(functools.partial(kernel, nb, nd, wx, wy), out_shape=(jax....  64.9 us
    unnamed x4, local copies, waits for them, and re-layouts  3.76 us

profile of v2, /device:TPU:1, one launch (start us, length us, event | category | flops | bytes accessed | tf_op | source)
XLA Modules:
  0.0 69.3 jit_solution(7807097596976147239)
XLA Ops:
  0.6 64.9 %sensitivity.1 = (f32[64,64,128]{2,1,0:T(8,128)}, f32[1,1024]{1,0:T(1,128)}) custom-call(bf16[27,27]{1,0:T(8,128)(2,1)} %coup.1, f32[1,1024]{1,0:T(1,128)} %bitcast.7, s32[1,1024]{1,0:T(1,128)} %bitcast.8, s32[1,1024]{1,0:T(1,128)} %bitcast.9, bf16[3,27,1024]{2,1,0:T(8,128)(2,1)} %vel_h.1, bf16[3,27,1024]{2,1,0:T(8,128)(2,1)} %adj_h.1, s32[128,1024]{1,0:T(8,128)} %off_h.1, ...), custom_call_target="tpu_custom_call" | custom-call | tf_op jit(solution)/shard_map/sensitivity/pallas_call | solution.py:374
  65.6 0.0 copy-start
  65.6 3.2 %copy.13 = f32[64,64,128]{2,1,0:T(8,128)} copy(f32[64,64,128]{2,1,0:T(8,128)} %get-tuple-element.8) | data formatting | bytes 4194304
  68.7 0.0 copy-done
  68.7 0.6 copy.14
Async XLA Ops:
  65.6 3.2 %copy-start = (f32[1,1024]{1,0:T(1,128)S(1)}, f32[1,1024]{1,0:T(1,128)}, u32[]{:S(2)}) copy-start(f32[1,1024]{1,0:T(1,128)} %get-tuple-element.5) | copy-start | bytes 12292

commit v3 on v2

--- a/solution.py
+++ b/solution.py
@@ -63,10 +63,21 @@
     groups = ndev // gsrc
     brick = lax.axis_index("brick")
     dom = lax.axis_index("dom")
-    me = brick * nd + dom
-
-    def dev(lin):
-        return (lin // nd, lin % nd)
+
+    def ahead(db, dd):
+        return (brick + db) & (nb - 1), (dom + dd) & (nd - 1)
+
+    def behind(db, dd):
+        return (brick - db) & (nb - 1), (dom - dd) & (nd - 1)
+
+    def others_in_turn(act):
+        @pl.loop(1, nb)
+        def _(i):
+            for dd in reversed(range(nd)):
+                act(nb - i, dd)
+
+        for dd in reversed(range(1, nd)):
+            act(0, dd)
 
     loads = [
         pltpu.make_async_copy(h, v, in_sem.at[i])
@@ -77,13 +88,13 @@
 
     barrier = pltpu.get_barrier_semaphore()
 
-    @pl.loop(1, ndev)
-    def _(i):
-        pl.semaphore_signal(
-            barrier, inc=1, device_id=dev((me + (ndev - i)) % ndev), device_id_type=MESH
-        )
-
-    rel = (own[...] - me + ndev) % ndev
+    def greet(db, dd):
+        pl.semaphore_signal(barrier, inc=1, device_id=ahead(db, dd), device_id_type=MESH)
+
+    others_in_turn(greet)
+
+    owners = own[...]
+    rel = ((owners // nd - brick) & (nb - 1)) * nd + ((owners % nd - dom) & (nd - 1))
     rr = iota((LANES, 2 * LANES), 0)
     cc = iota((LANES, 2 * LANES), 1)
     upper = onehot((rr < cc) | (cc >= LANES)).astype(BF16)
@@ -152,51 +163,48 @@
 
         zero = jnp.zeros((8, LANES), F32)
         built = jnp.concatenate(lax.fori_loop(0, entries // 8, slot8, (zero,) * tiles), axis=0)
-        hi, lo = split2(built)
-        wt[0:LANES, sl] = hi
-        wt[LANES : 2 * LANES, sl] = lo
-
-    prows = min(slots, 512)
-
-    @pl.loop(0, slots // prows)
-    def _(g):
-        start = pl.multiple_of(g * prows, prows)
-        pick = onehot(placed == iota((prows, count), 0) + start).astype(BF16)
-        both = mm(pick, wt[...], NT)
-        send[pl.ds(start, prows), :] = both[:, :LANES] + both[:, LANES:]
+        hi, lo = split2(built.T)
+        wt[sl, 0:LANES] = hi
+        wt[sl, LANES : 2 * LANES] = lo
+
+    pick = onehot(placed == iota((slots, count), 0)).astype(BF16)
+    both = mm(pick, wt[...])
+    send[...] = both[:, :LANES] + both[:, LANES:]
 
     loads[4].wait()
+
+    pl.semaphore_wait(barrier, ndev - 1)
+
+    def row_copy(src, dst, send_sem, recv_sem, to):
+        return pltpu.make_async_remote_copy(
+            src_ref=src, dst_ref=dst, send_sem=send_sem, recv_sem=recv_sem,
+            device_id=to, device_id_type=MESH,
+        )
+
+    pltpu.make_async_copy(msend.at[pl.ds(0, 1)], mrecv.at[pl.ds(0, 1)], mrsem).start()
+
+    def send_meta(db, dd):
+        row = pl.ds(db * nd + dd, 1)
+        row_copy(msend.at[row], mrecv.at[row], msem, mrsem, ahead(db, dd)).start()
+
+    others_in_turn(send_meta)
+
+    own_rows = pl.ds(0, CAP)
+    pltpu.make_async_copy(send.at[own_rows], recv.at[own_rows], rsem.at[0]).start()
+
+    def send_maps(db, dd):
+        at = pl.ds(pl.multiple_of((db * nd + dd) * CAP, CAP), CAP)
+        row_copy(
+            send.at[at], recv.at[at], ssem, rsem.at[db * nd // gsrc], ahead(db, dd)
+        ).start()
+
+    others_in_turn(send_maps)
 
     @pl.loop(0, wx)
     def _(x):
         at = pl.ds(pl.multiple_of(x * wy, wy), wy)
         th[at, :] = jnp.tanh(SHARP * (th[at, :] - THRESHOLD))
         acc[at, :] = jnp.zeros((wy, LANES), F32)
-
-    pl.semaphore_wait(barrier, ndev - 1)
-
-    def row_copy(src, dst, send_sem, recv_sem, lin):
-        return pltpu.make_async_remote_copy(
-            src_ref=src, dst_ref=dst, send_sem=send_sem, recv_sem=recv_sem,
-            device_id=dev(lin), device_id_type=MESH,
-        )
-
-    pltpu.make_async_copy(msend.at[pl.ds(0, 1)], mrecv.at[pl.ds(0, 1)], mrsem).start()
-
-    @pl.loop(1, ndev)
-    def _(i):
-        j = ndev - i
-        row = pl.ds(j, 1)
-        row_copy(msend.at[row], mrecv.at[row], msem, mrsem, (me + j) % ndev).start()
-
-    own_rows = pl.ds(0, CAP)
-    pltpu.make_async_copy(send.at[own_rows], recv.at[own_rows], rsem.at[0]).start()
-
-    @pl.loop(1, ndev)
-    def _(i):
-        j = ndev - i
-        at = pl.ds(pl.multiple_of(j * CAP, CAP), CAP)
-        row_copy(send.at[at], recv.at[at], ssem, rsem.at[j // gsrc], (me + j) % ndev).start()
 
     pltpu.make_async_copy(mrecv, mrecv, mrsem).wait()
     got = mrecv[...]
@@ -213,13 +221,11 @@
         line = jnp.sum(jnp.where(eye, p_lines[c : c + 1], 0.0), axis=1, keepdims=True)
         pcol[c * LANES : (c + 1) * LANES, :] = jnp.broadcast_to(line, (LANES, LANES))
 
-    @pl.loop(0, slots // 8)
-    def _(r8):
-        c = r8 // 16
-        l0 = (r8 % 16) * 8
-        for k in range(8):
-            at = jnp.minimum(jnp.maximum(ids_s[c, l0 + k], 0), voxel_rows - 1)
-            rows[pl.ds(pl.multiple_of(r8 * 8, 8) + k, 1), :] = th[pl.ds(at, 1), :]
+    @pl.loop(0, slots // LANES)
+    def _(c):
+        for k in range(LANES):
+            at = ids_s[c, k] & (voxel_rows - 1)
+            rows[pl.ds(c * LANES + k, 1), :] = th[pl.ds(at, 1), :]
 
     yrow = iota((wy, grows), 0)
 
@@ -245,20 +251,17 @@
         xid = idr // wy
         yhot = onehot(yrow == idr % wy)
 
-        @pl.loop(0, gsrc)
-        def _(q):
-            j = g * gsrc + q
-            c = j // 8
-
-            @pl.when(j > 0)
-            def _():
-                row_copy(
-                    dsend.at[pl.ds(c, 1)], drecv.at[pl.ds(j, 1)], dsem, drsem, (me + (ndev - j)) % ndev
-                ).start()
-
-            @pl.when(j == 0)
-            def _():
-                pltpu.make_async_copy(dsend.at[pl.ds(c, 1)], drecv.at[pl.ds(j, 1)], drsem).start()
+        for q in range(gsrc):
+            db = g * (gsrc // nd) + q // nd
+            dd = q % nd
+            c = g * (gsrc // 8) + q // 8
+            back = row_copy(
+                dsend.at[pl.ds(c, 1)], drecv.at[pl.ds(g * gsrc + q, 1)], dsem, drsem, behind(db, dd)
+            )
+            if q:
+                back.start()
+            else:
+                pl.when(g > 0)(back.start)
 
         pick = jnp.concatenate([jnp.where(xid == x, yhot, 0.0) for x in range(wx)], axis=0)
         added = mm(pick.astype(BF16), both)
@@ -292,22 +295,6 @@
     ]
     for halo in halos:
         halo.start()
-    for halo in halos:
-        halo.wait()
-
-    for edge, first_x in ((brick == 0, 0), (brick == nb - 1, wx + 2)):
-
-        @pl.when(edge)
-        def _():
-            ext[first_x : first_x + 2] = jnp.zeros((2, ext.shape[1], LANES), F32)
-
-    for edge, first_y in ((dom == 0, YO - 2), (dom == nd - 1, YO + wy)):
-
-        @pl.when(edge)
-        def _():
-            @pl.loop(0, wx + 4)
-            def _(x):
-                ext[x, first_y : first_y + 2, :] = jnp.zeros((2, LANES), F32)
 
     tall = fst.shape[1]
 
@@ -320,15 +307,52 @@
         total = total + jnp.where(zline == LANES - 1, 0.0, pltpu.roll(y, LANES - 1, axis=1))
         return y, total
 
-    line = iota((tall, LANES), 0)
-    inside = (line >= jnp.where(dom == 0, 1, 0)) & (line <= jnp.where(dom == nd - 1, wy, wy + 1))
-
-    @pl.loop(0, (wx + 2) // 2)
-    def _(half):
-        for u in range(2):
-            x = half * 2 + u + 1
-            y, near = around(ext, x, YO - 1, tall)
-            fst[x] = jnp.where(inside, 0.19 * y + 0.135 * near, 0.0)
+    def first_sweep(x, row, size):
+        y, near = around(ext, x, YO - 1 + row, size)
+        fst[x, row : row + size, :] = 0.19 * y + 0.135 * near
+
+    def in_steps(start, stop, step, act):
+        @pl.loop(0, (stop - start) // step)
+        def _(i):
+            for u in range(step):
+                act(start + i * step + u)
+
+        for x in range(start + (stop - start) // step * step, stop):
+            act(x)
+
+    in_steps(3, wx + 1, 4, lambda x: first_sweep(x, 8, wy - 8))
+    for halo in halos:
+        halo.wait()
+
+    for edge, first_x in ((brick == 0, 0), (brick == nb - 1, wx + 2)):
+
+        @pl.when(edge)
+        def _():
+            ext[first_x : first_x + 2] = jnp.zeros((2, ext.shape[1], LANES), F32)
+
+    for edge, first_y in ((dom == 0, YO - 2), (dom == nd - 1, YO + wy)):
+
+        @pl.when(edge)
+        def _():
+            @pl.loop(0, wx + 4)
+            def _(x):
+                ext[x, first_y : first_y + 2, :] = jnp.zeros((2, LANES), F32)
+
+    def rims(x):
+        first_sweep(x, 0, 8)
+        first_sweep(x, wy, 8)
+
+    for x in (1, 2, wx + 1, wx + 2):
+        first_sweep(x, 0, tall)
+    in_steps(3, wx + 1, 4, rims)
+
+    for edge, row in ((dom == 0, 0), (dom == nd - 1, wy + 1)):
+
+        @pl.when(edge)
+        def _():
+            @pl.loop(1, wx + 3)
+            def _(x):
+                fst[x, row : row + 1, :] = jnp.zeros((1, LANES), F32)
 
     for edge, first_x in ((brick == 0, 1), (brick == nb - 1, wx + 2)):
 
@@ -336,15 +360,16 @@
         def _():
             fst[first_x] = jnp.zeros((tall, LANES), F32)
 
-    @pl.loop(0, wx // 2)
-    def _(half):
-        for u in range(2):
-            x = half * 2 + u
-            y, near = around(fst, x + 2, 1, wy)
-            out[x] = 0.1 * y + 0.09 * ext[x + 2, YO : YO + wy, :] + 0.135 * near
+    def second_sweep(x):
+        y, near = around(fst, x + 2, 1, wy)
+        out[x] = 0.1 * y + 0.09 * ext[x + 2, YO : YO + wy, :] + 0.135 * near
+
+    in_steps(0, wx, 4, second_sweep)
 
     store = pltpu.make_async_copy(out, res_h, osem)
     store.start()
+
+    pltpu.make_async_copy(dsend.at[pl.ds(0, 1)], drecv.at[pl.ds(0, 1)], drsem).start()
 
     pltpu.make_async_copy(drecv, drecv, drsem).wait()
     back = jnp.where(is_id, drecv[...], 0.0).T
@@ -354,10 +379,10 @@
     den[...] = jnp.sum(jnp.where(kmask, spread, 0.0), axis=0, keepdims=True)
 
     others = pl.ds(1, ndev - 1)
-    row_copy(msend.at[others], mrecv.at[others], msem, mrsem, me).wait_send()
+    row_copy(msend.at[others], mrecv.at[others], msem, mrsem, (brick, dom)).wait_send()
     most = pl.ds(CAP, slots - CAP)
-    row_copy(send.at[most], recv.at[most], ssem, rsem.at[0], me).wait_send()
-    row_copy(drecv.at[others], drecv.at[others], dsem, drsem, me).wait_send()
+    row_copy(send.at[most], recv.at[most], ssem, rsem.at[0], (brick, dom)).wait_send()
+    row_copy(drecv.at[others], drecv.at[others], dsem, drsem, (brick, dom)).wait_send()
     store.wait()
 
 
@@ -387,7 +412,7 @@
             pltpu.VMEM((wx * wy, LANES), F32),
             pltpu.VMEM((ndev, count), BF16),
             pltpu.VMEM((1, count), F32),
-            pltpu.VMEM((2 * LANES, count), BF16),
+            pltpu.VMEM((count, 2 * LANES), BF16),
             pltpu.VMEM((offsets.shape[0], LANES), jnp.int32),
             pltpu.VMEM((LANES // 8, offsets.shape[0], LANES), F32),
             pltpu.VMEM((ndev, LANES), F32),

time: 69.5 us -> 56.1 us (0.81)
  Pallas kernels: 64.9 us -> 51.4 us
    pallas_call x1, Pallas kernels: 64.9 us -> 51.4 us  [body(): pl.pallas_call(functools.partial(kernel, nb, nd, wx, wy), out_shape=(jax....]
where the time goes in v3:
time: 56.1 us; the launch traced here: 55.8 us
  Pallas kernels  51.4 us (92%)
  local copies, waits for them, and re-layouts  3.76 us (7%)
  between operations  0.65 us (1%)
    pallas_call x1, Pallas kernels, body(): pl.pallas_call(functools.partial(kernel, nb, nd, wx, wy), out_shape=(jax....  51.4 us
    unnamed x4, local copies, waits for them, and re-layouts  3.76 us

profile of v3, /device:TPU:1, one launch (start us, length us, event | category | flops | bytes accessed | tf_op | source)
XLA Modules:
  0.0 55.8 jit_solution(14956474645245909196)
XLA Ops:
  0.6 51.4 %sensitivity.1 = (f32[64,64,128]{2,1,0:T(8,128)}, f32[1,1024]{1,0:T(1,128)}) custom-call(bf16[27,27]{1,0:T(8,128)(2,1)} %coup.1, f32[1,1024]{1,0:T(1,128)} %bitcast.7, s32[1,1024]{1,0:T(1,128)} %bitcast.8, s32[1,1024]{1,0:T(1,128)} %bitcast.9, bf16[3,27,1024]{2,1,0:T(8,128)(2,1)} %vel_h.1, bf16[3,27,1024]{2,1,0:T(8,128)(2,1)} %adj_h.1, s32[128,1024]{1,0:T(8,128)} %off_h.1, ...), custom_call_target="tpu_custom_call" | custom-call | tf_op jit(solution)/shard_map/sensitivity/pallas_call | solution.py:399
  52.0 0.0 copy-start
  52.0 3.2 %copy.13 = f32[64,64,128]{2,1,0:T(8,128)} copy(f32[64,64,128]{2,1,0:T(8,128)} %get-tuple-element.8) | data formatting | bytes 4194304
  55.2 0.0 copy-done
  55.2 0.6 %copy.14 = f32[1024]{0:T(1024)} copy(f32[1024]{0:T(1024)S(1)} %bitcast.6) | data formatting | bytes 8192
Async XLA Ops:
  52.0 3.2 %copy-start = (f32[1,1024]{1,0:T(1,128)S(1)}, f32[1,1024]{1,0:T(1,128)}, u32[]{:S(2)}) copy-start(f32[1,1024]{1,0:T(1,128)} %get-tuple-element.5) | copy-start | bytes 12292

commit v4 on v3

--- a/solution.py
+++ b/solution.py
@@ -58,26 +58,38 @@
     blocks = count // LANES
     voxel_rows = wx * wy
     slots = ndev * CAP
-    gsrc = 16
+    xn, zn, yn = nb // 2, nd // 4, 4
+    gsrc = xn * yn
     grows = gsrc * CAP
-    groups = ndev // gsrc
+    groups = 2 * zn
     brick = lax.axis_index("brick")
     dom = lax.axis_index("dom")
-
-    def ahead(db, dd):
-        return (brick + db) & (nb - 1), (dom + dd) & (nd - 1)
-
-    def behind(db, dd):
-        return (brick - db) & (nb - 1), (dom - dd) & (nd - 1)
+    xi, ci, zi, yi = brick // 2, brick % 2, dom // yn, dom % yn
+
+    def ahead(g, m):
+        p, q = m // yn, m % yn
+        r = p + q + (g & (zn - 1))
+        return (
+            ((xi + p) & (xn - 1)) * 2 + ((ci + g // zn) & 1),
+            ((zi + r) & (zn - 1)) * yn + ((yi + q) & (yn - 1)),
+        )
+
+    def behind(g, m):
+        p, q = m // yn, m % yn
+        r = p + q + (g & (zn - 1))
+        return (
+            ((xi - p) & (xn - 1)) * 2 + ((ci - g // zn) & 1),
+            ((zi - r) & (zn - 1)) * yn + ((yi - q) & (yn - 1)),
+        )
 
     def others_in_turn(act):
-        @pl.loop(1, nb)
+        @pl.loop(1, groups)
         def _(i):
-            for dd in reversed(range(nd)):
-                act(nb - i, dd)
-
-        for dd in reversed(range(1, nd)):
-            act(0, dd)
+            for m in reversed(range(gsrc)):
+                act(groups - i, m)
+
+        for m in reversed(range(1, gsrc)):
+            act(0, m)
 
     loads = [
         pltpu.make_async_copy(h, v, in_sem.at[i])
@@ -88,13 +100,17 @@
 
     barrier = pltpu.get_barrier_semaphore()
 
-    def greet(db, dd):
-        pl.semaphore_signal(barrier, inc=1, device_id=ahead(db, dd), device_id_type=MESH)
+    def greet(g, m):
+        pl.semaphore_signal(barrier, inc=1, device_id=ahead(g, m), device_id_type=MESH)
 
     others_in_turn(greet)
 
     owners = own[...]
-    rel = ((owners // nd - brick) & (nb - 1)) * nd + ((owners % nd - dom) & (nd - 1))
+    obrick, odom = owners // nd, owners % nd
+    op = (obrick // 2 - xi) & (xn - 1)
+    oq = (odom % yn - yi) & (yn - 1)
+    ok = (odom // yn - zi - op - oq) & (zn - 1)
+    rel = ((((obrick % 2 - ci) & 1) * zn + ok) * xn + op) * yn + oq
     rr = iota((LANES, 2 * LANES), 0)
     cc = iota((LANES, 2 * LANES), 1)
     upper = onehot((rr < cc) | (cc >= LANES)).astype(BF16)
@@ -141,13 +157,13 @@
     for b in range(blocks):
         sl = slice(b * LANES, (b + 1) * LANES)
 
-        @pl.loop(0, entries // 8)
+        @pl.loop(0, entries // 8, unroll=2)
         def _(i):
             at = pl.ds(pl.multiple_of(i * 8, 8), 8)
             o8 = off[at, sl]
             m8 = mar[at, sl]
-            fine[at, :] = o8 % 8
-            tile = o8 // 8
+            fine[at, :] = o8 & 7
+            tile = o8 >> 3
             for u in range(tiles):
                 parts[u, at, :] = jnp.where(tile == u, m8, 0.0)
 
@@ -162,7 +178,7 @@
             return tuple(totals)
 
         zero = jnp.zeros((8, LANES), F32)
-        built = jnp.concatenate(lax.fori_loop(0, entries // 8, slot8, (zero,) * tiles), axis=0)
+        built = jnp.concatenate(lax.fori_loop(0, entries // 8, slot8, (zero,) * tiles, unroll=2), axis=0)
         hi, lo = split2(built.T)
         wt[sl, 0:LANES] = hi
         wt[sl, LANES : 2 * LANES] = lo
@@ -183,20 +199,18 @@
 
     pltpu.make_async_copy(msend.at[pl.ds(0, 1)], mrecv.at[pl.ds(0, 1)], mrsem).start()
 
-    def send_meta(db, dd):
-        row = pl.ds(db * nd + dd, 1)
-        row_copy(msend.at[row], mrecv.at[row], msem, mrsem, ahead(db, dd)).start()
+    def send_meta(g, m):
+        row = pl.ds(g * gsrc + m, 1)
+        row_copy(msend.at[row], mrecv.at[row], msem, mrsem, ahead(g, m)).start()
 
     others_in_turn(send_meta)
 
     own_rows = pl.ds(0, CAP)
     pltpu.make_async_copy(send.at[own_rows], recv.at[own_rows], rsem.at[0]).start()
 
-    def send_maps(db, dd):
-        at = pl.ds(pl.multiple_of((db * nd + dd) * CAP, CAP), CAP)
-        row_copy(
-            send.at[at], recv.at[at], ssem, rsem.at[db * nd // gsrc], ahead(db, dd)
-        ).start()
+    def send_maps(g, m):
+        at = pl.ds(pl.multiple_of((g * gsrc + m) * CAP, CAP), CAP)
+        row_copy(send.at[at], recv.at[at], ssem, rsem.at[g], ahead(g, m)).start()
 
     others_in_turn(send_maps)
 
@@ -252,11 +266,9 @@
         yhot = onehot(yrow == idr % wy)
 
         for q in range(gsrc):
-            db = g * (gsrc // nd) + q // nd
-            dd = q % nd
             c = g * (gsrc // 8) + q // 8
             back = row_copy(
-                dsend.at[pl.ds(c, 1)], drecv.at[pl.ds(g * gsrc + q, 1)], dsem, drsem, behind(db, dd)
+                dsend.at[pl.ds(c, 1)], drecv.at[pl.ds(g * gsrc + q, 1)], dsem, drsem, behind(g, q)
             )
             if q:
                 back.start()
@@ -320,7 +332,7 @@
         for x in range(start + (stop - start) // step * step, stop):
             act(x)
 
-    in_steps(3, wx + 1, 4, lambda x: first_sweep(x, 8, wy - 8))
+    in_steps(3, wx + 1, 8, lambda x: first_sweep(x, 8, wy - 8))
     for halo in halos:
         halo.wait()
 
@@ -344,7 +356,7 @@
 
     for x in (1, 2, wx + 1, wx + 2):
         first_sweep(x, 0, tall)
-    in_steps(3, wx + 1, 4, rims)
+    in_steps(3, wx + 1, 8, rims)
 
     for edge, row in ((dom == 0, 0), (dom == nd - 1, wy + 1)):
 
@@ -364,10 +376,15 @@
         y, near = around(fst, x + 2, 1, wy)
         out[x] = 0.1 * y + 0.09 * ext[x + 2, YO : YO + wy, :] + 0.135 * near
 
-    in_steps(0, wx, 4, second_sweep)
-
-    store = pltpu.make_async_copy(out, res_h, osem)
-    store.start()
+    half = wx // 2
+    stores = [
+        pltpu.make_async_copy(out.at[pl.ds(s * half, half)], res_h.at[pl.ds(s * half, half)], osem.at[s])
+        for s in range(2)
+    ]
+    for s in range(2):
+        in_steps(s * half, (s + 1) * half, 8, second_sweep)
+        stores[s].start()
+
 
     pltpu.make_async_copy(dsend.at[pl.ds(0, 1)], drecv.at[pl.ds(0, 1)], drsem).start()
 
@@ -383,7 +400,8 @@
     most = pl.ds(CAP, slots - CAP)
     row_copy(send.at[most], recv.at[most], ssem, rsem.at[0], (brick, dom)).wait_send()
     row_copy(drecv.at[others], drecv.at[others], dsem, drsem, (brick, dom)).wait_send()
-    store.wait()
+    for store in stores:
+        store.wait()
 
 
 def body(velocity, adjoint, coupling, jac_weight, owner, local_block, offsets, margin, filtered):
@@ -429,7 +447,7 @@
             pltpu.VMEM((wx + 4, wide, LANES), F32),
             pltpu.VMEM((wx + 4, wy + 8, LANES), F32),
             pltpu.VMEM(filtered.shape, F32),
-            dma((5,)), dma, dma, dma, dma, dma((ndev // 16,)), dma, dma, dma((8,)), dma((8,)), dma,
+            dma((5,)), dma, dma, dma, dma, dma((nd // 2,)), dma, dma, dma((8,)), dma((8,)), dma((2,)),
         ],
         compiler_params=pltpu.CompilerParams(
             collective_id=0, has_side_effects=True, vmem_limit_bytes=60 * 1024 * 1024

time: 56.1 us -> 51.4 us (0.916)
  Pallas kernels: 51.4 us -> 46.8 us
    pallas_call x1, Pallas kernels: 51.4 us -> 46.8 us  [body(): pl.pallas_call(functools.partial(kernel, nb, nd, wx, wy), out_shape=(jax....]
where the time goes in v4:
time: 51.4 us; the launch traced here: 51.2 us
  Pallas kernels  46.8 us (91%)
  local copies, waits for them, and re-layouts  3.76 us (7%)
  between operations  0.65 us (1%)
    pallas_call x1, Pallas kernels, body(): pl.pallas_call(functools.partial(kernel, nb, nd, wx, wy), out_shape=(jax....  46.8 us
    unnamed x4, local copies, waits for them, and re-layouts  3.76 us

profile of v4, /device:TPU:1, one launch (start us, length us, event | category | flops | bytes accessed | tf_op | source)
XLA Modules:
  0.0 51.2 jit_solution(5372756695623634367)
XLA Ops:
  0.6 46.8 %sensitivity.1 = (f32[64,64,128]{2,1,0:T(8,128)}, f32[1,1024]{1,0:T(1,128)}) custom-call(bf16[27,27]{1,0:T(8,128)(2,1)} %coup.1, f32[1,1024]{1,0:T(1,128)} %bitcast.7, s32[1,1024]{1,0:T(1,128)} %bitcast.8, s32[1,1024]{1,0:T(1,128)} %bitcast.9, bf16[3,27,1024]{2,1,0:T(8,128)(2,1)} %vel_h.1, bf16[3,27,1024]{2,1,0:T(8,128)(2,1)} %adj_h.1, s32[128,1024]{1,0:T(8,128)} %off_h.1, ...), custom_call_target="tpu_custom_call" | custom-call | tf_op jit(solution)/shard_map/sensitivity/pallas_call | solution.py:417
  47.5 0.0 copy-start
  47.5 3.2 %copy.13 = f32[64,64,128]{2,1,0:T(8,128)} copy(f32[64,64,128]{2,1,0:T(8,128)} %get-tuple-element.8) | data formatting | bytes 4194304
  50.6 0.0 copy-done
  50.6 0.6 %copy.14 = f32[1024]{0:T(1024)} copy(f32[1024]{0:T(1024)S(1)} %bitcast.6) | data formatting | bytes 8192
Async XLA Ops:
  47.5 3.2 %copy-start = (f32[1,1024]{1,0:T(1,128)S(1)}, f32[1,1024]{1,0:T(1,128)}, u32[]{:S(2)}) copy-start(f32[1,1024]{1,0:T(1,128)} %get-tuple-element.5) | copy-start | bytes 12292

commit v5 on v4

--- a/solution.py
+++ b/solution.py
@@ -47,9 +47,9 @@
 
 
 def kernel(
-    nb, nd, wx, wy, coup, jac, own, loc, vel_h, adj_h, off_h, mar_h, fil_h,
+    nb, nd, wx, wy, coup_h, jac_h, own_h, loc_h, vel_h, adj_h, off_h, mar_h, fil_h,
     res_h, den,
-    vel, adj, off, mar, th, mt, pos, wt, fine, parts, msend, mrecv, send, recv, ids_v, ids_s, pcol,
+    coup, jac, own, loc, vel, adj, off, mar, th, mt, pos, wt, fine, parts, msend, mrecv, send, recv, ids_v, ids_s, pcol,
     rows, acc, dsend, drecv, ext, fst, out,
     in_sem, smem_sem, msem, mrsem, ssem, rsem, dsem, drsem, hsem, hrsem, osem,
 ):
@@ -82,20 +82,24 @@
             ((zi - r) & (zn - 1)) * yn + ((yi - q) & (yn - 1)),
         )
 
-    def others_in_turn(act):
-        @pl.loop(1, groups)
+    def others_in_turn(act, low, high):
+        @pl.loop(0, high - max(low, 1))
         def _(i):
             for m in reversed(range(gsrc)):
-                act(groups - i, m)
-
-        for m in reversed(range(1, gsrc)):
-            act(0, m)
+                act(high - 1 - i, m)
+
+        if low == 0:
+            for m in reversed(range(1, gsrc)):
+                act(0, m)
 
     loads = [
         pltpu.make_async_copy(h, v, in_sem.at[i])
-        for i, (h, v) in enumerate(((vel_h, vel), (adj_h, adj), (off_h, off), (mar_h, mar), (fil_h, th)))
+        for i, (h, v) in enumerate((
+            (vel_h, vel), (adj_h, adj), (off_h, off), (mar_h, mar), (fil_h, th),
+            (coup_h, coup), (jac_h, jac), (loc_h, loc), (own_h, own),
+        ))
     ]
-    for load in loads:
+    for load in reversed(loads):
         load.start()
 
     barrier = pltpu.get_barrier_semaphore()
@@ -103,8 +107,9 @@
     def greet(g, m):
         pl.semaphore_signal(barrier, inc=1, device_id=ahead(g, m), device_id_type=MESH)
 
-    others_in_turn(greet)
-
+    others_in_turn(greet, 0, groups)
+
+    loads[8].wait()
     owners = own[...]
     obrick, odom = owners // nd, owners % nd
     op = (obrick // 2 - xi) & (xn - 1)
@@ -126,8 +131,8 @@
     posi = pos[...].astype(jnp.int32)
     placed = rel * CAP + posi
 
-    loads[0].wait()
-    loads[1].wait()
+    for load in (*loads[:2], *loads[5:8]):
+        load.wait()
     total = None
     for c in range(3):
         part = vel[c].astype(F32) * mm(coup[...], adj[c])
@@ -167,27 +172,24 @@
             for u in range(tiles):
                 parts[u, at, :] = jnp.where(tile == u, m8, 0.0)
 
-        def slot8(i, totals):
-            totals = list(totals)
-            for k in range(8):
-                row = pl.ds(i * 8 + k, 1)
-                hit = jnp.broadcast_to(fine[row, :], (8, LANES)) == sub
-                for u in range(tiles):
-                    part = jnp.broadcast_to(parts[u, row, :], (8, LANES))
-                    totals[u] = totals[u] + jnp.where(hit, part, 0.0)
-            return tuple(totals)
-
-        zero = jnp.zeros((8, LANES), F32)
-        built = jnp.concatenate(lax.fori_loop(0, entries // 8, slot8, (zero,) * tiles, unroll=2), axis=0)
+        def summed(first):
+            def slot8(i, totals):
+                totals = list(totals)
+                for k in range(8):
+                    row = pl.ds(i * 8 + k, 1)
+                    hit = jnp.broadcast_to(fine[row, :], (8, LANES)) == sub
+                    for u in range(tiles // 2):
+                        part = jnp.broadcast_to(parts[first + u, row, :], (8, LANES))
+                        totals[u] = totals[u] + jnp.where(hit, part, 0.0)
+                return tuple(totals)
+
+            zero = jnp.zeros((8, LANES), F32)
+            return lax.fori_loop(0, entries // 8, slot8, (zero,) * (tiles // 2), unroll=2)
+
+        built = jnp.concatenate(summed(0) + summed(tiles // 2), axis=0)
         hi, lo = split2(built.T)
         wt[sl, 0:LANES] = hi
         wt[sl, LANES : 2 * LANES] = lo
-
-    pick = onehot(placed == iota((slots, count), 0)).astype(BF16)
-    both = mm(pick, wt[...])
-    send[...] = both[:, :LANES] + both[:, LANES:]
-
-    loads[4].wait()
 
     pl.semaphore_wait(barrier, ndev - 1)
 
@@ -203,16 +205,22 @@
         row = pl.ds(g * gsrc + m, 1)
         row_copy(msend.at[row], mrecv.at[row], msem, mrsem, ahead(g, m)).start()
 
-    others_in_turn(send_meta)
-
-    own_rows = pl.ds(0, CAP)
-    pltpu.make_async_copy(send.at[own_rows], recv.at[own_rows], rsem.at[0]).start()
+    others_in_turn(send_meta, 0, groups)
 
     def send_maps(g, m):
         at = pl.ds(pl.multiple_of((g * gsrc + m) * CAP, CAP), CAP)
         row_copy(send.at[at], recv.at[at], ssem, rsem.at[g], ahead(g, m)).start()
 
-    others_in_turn(send_maps)
+    for low, high in ((groups // 2, groups), (0, groups // 2)):
+        start, size = low * grows, (high - low) * grows
+        pick = onehot(placed == iota((size, count), 0) + start).astype(BF16)
+        both = mm(pick, wt[...])
+        send[start : start + size, :] = both[:, :LANES] + both[:, LANES:]
+        others_in_turn(send_maps, low, high)
+
+    own_rows = pl.ds(0, CAP)
+    pltpu.make_async_copy(send.at[own_rows], recv.at[own_rows], rsem.at[0]).start()
+    loads[4].wait()
 
     @pl.loop(0, wx)
     def _(x):
@@ -279,11 +287,27 @@
         added = mm(pick.astype(BF16), both)
         acc[...] = acc[...] + (added[:, :LANES] + added[:, LANES:])
 
-    @pl.loop(0, wx)
-    def _(x):
-        at = pl.ds(pl.multiple_of(x * wy, wy), wy)
+    def in_steps(start, stop, step, act):
+        @pl.loop(0, (stop - start) // step)
+        def _(i):
+            for u in range(step):
+                act(start + i * step + u)
+
+        for x in range(start + (stop - start) // step * step, stop):
+            act(x)
+
+    def source(x, row, size):
+        at = pl.ds(pl.multiple_of(x * wy + row, 8), size)
         t = th[at, :]
-        ext[x + 2, YO : YO + wy, :] = acc[at, :] * ((SHARP / (2.0 * T0)) * (1.0 - t * t))
+        ext[x + 2, YO + row : YO + row + size, :] = acc[at, :] * ((SHARP / (2.0 * T0)) * (1.0 - t * t))
+
+    def source_rims(x):
+        source(x, 0, 8)
+        source(x, wy - 8, 8)
+
+    in_steps(0, wx, 8, source_rims)
+    for x in (0, 1, wx - 2, wx - 1):
+        source(x, 8, wy - 16)
 
     xl, xh = (brick + (nb - 1)) % nb, (brick + 1) % nb
     yl, yh = (dom + (nd - 1)) % nd, (dom + 1) % nd
@@ -308,6 +332,7 @@
     for halo in halos:
         halo.start()
 
+    in_steps(2, wx - 2, 6, lambda x: source(x, 8, wy - 16))
     tall = fst.shape[1]
 
     def around(ref, x, y0, size):
@@ -322,15 +347,6 @@
     def first_sweep(x, row, size):
         y, near = around(ext, x, YO - 1 + row, size)
         fst[x, row : row + size, :] = 0.19 * y + 0.135 * near
-
-    def in_steps(start, stop, step, act):
-        @pl.loop(0, (stop - start) // step)
-        def _(i):
-            for u in range(step):
-                act(start + i * step + u)
-
-        for x in range(start + (stop - start) // step * step, stop):
-            act(x)
 
     in_steps(3, wx + 1, 8, lambda x: first_sweep(x, 8, wy - 8))
     for halo in halos:
@@ -420,9 +436,13 @@
             jax.ShapeDtypeStruct(filtered.shape, F32),
             jax.ShapeDtypeStruct((1, count), F32),
         ),
-        in_specs=[vmem] * 4 + [hbm] * 5,
+        in_specs=[hbm] * 9,
         out_specs=(hbm, vmem),
         scratch_shapes=[
+            pltpu.VMEM(coupling.shape, BF16),
+            pltpu.VMEM((1, count), F32),
+            pltpu.VMEM((1, count), jnp.int32),
+            pltpu.VMEM((1, count), jnp.int32),
             pltpu.VMEM(velocity.shape, BF16),
             pltpu.VMEM(adjoint.shape, BF16),
             pltpu.VMEM(offsets.shape, jnp.int32),
@@ -447,7 +467,7 @@
             pltpu.VMEM((wx + 4, wide, LANES), F32),
             pltpu.VMEM((wx + 4, wy + 8, LANES), F32),
             pltpu.VMEM(filtered.shape, F32),
-            dma((5,)), dma, dma, dma, dma, dma((nd // 2,)), dma, dma, dma((8,)), dma((8,)), dma((2,)),
+            dma((9,)), dma, dma, dma, dma, dma((nd // 2,)), dma, dma, dma((8,)), dma((8,)), dma((2,)),
         ],
         compiler_params=pltpu.CompilerParams(
             collective_id=0, has_side_effects=True, vmem_limit_bytes=60 * 1024 * 1024

time: 51.4 us -> 48.2 us (0.938)
  Pallas kernels: 46.8 us -> 43.6 us
    pallas_call x1, Pallas kernels: 46.8 us -> 43.6 us  [body(): pl.pallas_call(functools.partial(kernel, nb, nd, wx, wy), out_shape=(jax....]
where the time goes in v5:
time: 48.2 us; the launch traced here: 48 us
  Pallas kernels  43.6 us (90%)
  local copies, waits for them, and re-layouts  3.76 us (8%)
  between operations  0.65 us (1%)
    pallas_call x1, Pallas kernels, body(): pl.pallas_call(functools.partial(kernel, nb, nd, wx, wy), out_shape=(jax....  43.6 us
    unnamed x4, local copies, waits for them, and re-layouts  3.76 us

profile of v5, /device:TPU:1, one launch (start us, length us, event | category | flops | bytes accessed | tf_op | source)
XLA Modules:
  0.0 48.0 jit_solution(12983542491042427329)
XLA Ops:
  0.6 43.6 %sensitivity.1 = (f32[64,64,128]{2,1,0:T(8,128)}, f32[1,1024]{1,0:T(1,128)}) custom-call(bf16[27,27]{1,0:T(8,128)(2,1)} %coup_h.1, f32[1,1024]{1,0:T(1,128)} %bitcast.7, s32[1,1024]{1,0:T(1,128)} %bitcast.8, s32[1,1024]{1,0:T(1,128)} %bitcast.9, bf16[3,27,1024]{2,1,0:T(8,128)(2,1)} %vel_h.1, bf16[3,27,1024]{2,1,0:T(8,128)(2,1)} %adj_h.1, s32[128,1024]{1,0:T(8,128)} %off_h.1, ...), custom_call_target="tpu_custom_call" | custom-call | tf_op jit(solution)/shard_map/sensitivity/pallas_call | solution.py:433
  44.3 0.0 copy-start
  44.3 3.2 %copy.13 = f32[64,64,128]{2,1,0:T(8,128)} copy(f32[64,64,128]{2,1,0:T(8,128)} %get-tuple-element.8) | data formatting | bytes 4194304
  47.4 0.0 copy-done
  47.4 0.6 %copy.14 = f32[1024]{0:T(1024)} copy(f32[1024]{0:T(1024)S(1)} %bitcast.6) | data formatting | bytes 8192
Async XLA Ops:
  44.3 3.2 %copy-start = (f32[1,1024]{1,0:T(1,128)S(1)}, f32[1,1024]{1,0:T(1,128)}, u32[]{:S(2)}) copy-start(f32[1,1024]{1,0:T(1,128)} %get-tuple-element.5) | copy-start | bytes 12292

commit v6 on v5

--- a/solution.py
+++ b/solution.py
@@ -131,6 +131,64 @@
     posi = pos[...].astype(jnp.int32)
     placed = rel * CAP + posi
 
+    loads[2].wait()
+    loads[3].wait()
+    entries = off.shape[0]
+    tiles = LANES // 8
+    sub = iota((8, LANES), 0)
+    for b in range(blocks):
+        sl = slice(b * LANES, (b + 1) * LANES)
+
+        @pl.loop(0, entries // 8, unroll=2)
+        def _(i):
+            at = pl.ds(pl.multiple_of(i * 8, 8), 8)
+            o8 = off[at, sl]
+            m8 = mar[at, sl]
+            fine[at, :] = o8 & 7
+            tile = o8 >> 3
+            for u in range(tiles):
+                parts[u, at, :] = jnp.where(tile == u, m8, 0.0)
+
+        def summed(first):
+            def slot8(i, totals):
+                totals = list(totals)
+                for k in range(8):
+                    row = pl.ds(i * 8 + k, 1)
+                    hit = jnp.broadcast_to(fine[row, :], (8, LANES)) == sub
+                    for u in range(tiles // 2):
+                        part = jnp.broadcast_to(parts[first + u, row, :], (8, LANES))
+                        totals[u] = totals[u] + jnp.where(hit, part, 0.0)
+                return tuple(totals)
+
+            zero = jnp.zeros((8, LANES), F32)
+            return lax.fori_loop(0, entries // 8, slot8, (zero,) * (tiles // 2), unroll=2)
+
+        built = jnp.concatenate(summed(0) + summed(tiles // 2), axis=0)
+        hi, lo = split2(built.T)
+        wt[sl, 0:LANES] = hi
+        wt[sl, LANES : 2 * LANES] = lo
+
+    pl.semaphore_wait(barrier, ndev - 1)
+
+    def row_copy(src, dst, send_sem, recv_sem, to):
+        return pltpu.make_async_remote_copy(
+            src_ref=src, dst_ref=dst, send_sem=send_sem, recv_sem=recv_sem,
+            device_id=to, device_id_type=MESH,
+        )
+
+    def send_maps(g, m):
+        at = pl.ds(pl.multiple_of((g * gsrc + m) * CAP, CAP), CAP)
+        row_copy(send.at[at], recv.at[at], ssem, rsem.at[g], ahead(g, m)).start()
+
+    def place_and_send(low, high):
+        start, size = low * grows, (high - low) * grows
+        pick = onehot(placed == iota((size, count), 0) + start).astype(BF16)
+        both = mm(pick, wt[...])
+        send[start : start + size, :] = both[:, :LANES] + both[:, LANES:]
+        others_in_turn(send_maps, low, high)
+
+    place_and_send(groups // 2, groups)
+
     for load in (*loads[:2], *loads[5:8]):
         load.wait()
     total = None
@@ -154,51 +212,6 @@
     is_p = jlane == (jrow + 4) % 8
     msend[...] = jnp.where(is_id, id_rows, jnp.where(is_p, p_rows, 0.0))
 
-    loads[2].wait()
-    loads[3].wait()
-    entries = off.shape[0]
-    tiles = LANES // 8
-    sub = iota((8, LANES), 0)
-    for b in range(blocks):
-        sl = slice(b * LANES, (b + 1) * LANES)
-
-        @pl.loop(0, entries // 8, unroll=2)
-        def _(i):
-            at = pl.ds(pl.multiple_of(i * 8, 8), 8)
-            o8 = off[at, sl]
-            m8 = mar[at, sl]
-            fine[at, :] = o8 & 7
-            tile = o8 >> 3
-            for u in range(tiles):
-                parts[u, at, :] = jnp.where(tile == u, m8, 0.0)
-
-        def summed(first):
-            def slot8(i, totals):
-                totals = list(totals)
-                for k in range(8):
-                    row = pl.ds(i * 8 + k, 1)
-                    hit = jnp.broadcast_to(fine[row, :], (8, LANES)) == sub
-                    for u in range(tiles // 2):
-                        part = jnp.broadcast_to(parts[first + u, row, :], (8, LANES))
-                        totals[u] = totals[u] + jnp.where(hit, part, 0.0)
-                return tuple(totals)
-
-            zero = jnp.zeros((8, LANES), F32)
-            return lax.fori_loop(0, entries // 8, slot8, (zero,) * (tiles // 2), unroll=2)
-
-        built = jnp.concatenate(summed(0) + summed(tiles // 2), axis=0)
-        hi, lo = split2(built.T)
-        wt[sl, 0:LANES] = hi
-        wt[sl, LANES : 2 * LANES] = lo
-
-    pl.semaphore_wait(barrier, ndev - 1)
-
-    def row_copy(src, dst, send_sem, recv_sem, to):
-        return pltpu.make_async_remote_copy(
-            src_ref=src, dst_ref=dst, send_sem=send_sem, recv_sem=recv_sem,
-            device_id=to, device_id_type=MESH,
-        )
-
     pltpu.make_async_copy(msend.at[pl.ds(0, 1)], mrecv.at[pl.ds(0, 1)], mrsem).start()
 
     def send_meta(g, m):
@@ -207,16 +220,7 @@
 
     others_in_turn(send_meta, 0, groups)
 
-    def send_maps(g, m):
-        at = pl.ds(pl.multiple_of((g * gsrc + m) * CAP, CAP), CAP)
-        row_copy(send.at[at], recv.at[at], ssem, rsem.at[g], ahead(g, m)).start()
-
-    for low, high in ((groups // 2, groups), (0, groups // 2)):
-        start, size = low * grows, (high - low) * grows
-        pick = onehot(placed == iota((size, count), 0) + start).astype(BF16)
-        both = mm(pick, wt[...])
-        send[start : start + size, :] = both[:, :LANES] + both[:, LANES:]
-        others_in_turn(send_maps, low, high)
+    place_and_send(0, groups // 2)
 
     own_rows = pl.ds(0, CAP)
     pltpu.make_async_copy(send.at[own_rows], recv.at[own_rows], rsem.at[0]).start()
@@ -273,19 +277,19 @@
         xid = idr // wy
         yhot = onehot(yrow == idr % wy)
 
-        for q in range(gsrc):
+        def reply(q):
             c = g * (gsrc // 8) + q // 8
-            back = row_copy(
+            row_copy(
                 dsend.at[pl.ds(c, 1)], drecv.at[pl.ds(g * gsrc + q, 1)], dsem, drsem, behind(g, q)
-            )
-            if q:
-                back.start()
-            else:
-                pl.when(g > 0)(back.start)
+            ).start()
+
+        for q in range(1, gsrc):
+            reply(q)
 
         pick = jnp.concatenate([jnp.where(xid == x, yhot, 0.0) for x in range(wx)], axis=0)
         added = mm(pick.astype(BF16), both)
         acc[...] = acc[...] + (added[:, :LANES] + added[:, LANES:])
+        pl.when(g > 0)(lambda: reply(0))
 
     def in_steps(start, stop, step, act):
         @pl.loop(0, (stop - start) // step)

time: 48.2 us -> 51.9 us (1.077)
  Pallas kernels: 43.6 us -> 47.4 us
    pallas_call x1, Pallas kernels: 43.6 us -> 47.4 us  [body(): pl.pallas_call(functools.partial(kernel, nb, nd, wx, wy), out_shape=(jax....]
where the time goes in v6:
time: 51.9 us; the launch traced here: 51.8 us
  Pallas kernels  47.4 us (91%)
  local copies, waits for them, and re-layouts  3.76 us (7%)
  between operations  0.65 us (1%)
    pallas_call x1, Pallas kernels, body(): pl.pallas_call(functools.partial(kernel, nb, nd, wx, wy), out_shape=(jax....  47.4 us
    unnamed x4, local copies, waits for them, and re-layouts  3.76 us

profile of v6, /device:TPU:1, one launch (start us, length us, event | category | flops | bytes accessed | tf_op | source)
XLA Modules:
  0.0 51.8 jit_solution(15278084743162751383)
XLA Ops:
  0.6 47.4 %sensitivity.1 = (f32[64,64,128]{2,1,0:T(8,128)}, f32[1,1024]{1,0:T(1,128)}) custom-call(bf16[27,27]{1,0:T(8,128)(2,1)} %coup_h.1, f32[1,1024]{1,0:T(1,128)} %bitcast.7, s32[1,1024]{1,0:T(1,128)} %bitcast.8, s32[1,1024]{1,0:T(1,128)} %bitcast.9, bf16[3,27,1024]{2,1,0:T(8,128)(2,1)} %vel_h.1, bf16[3,27,1024]{2,1,0:T(8,128)(2,1)} %adj_h.1, s32[128,1024]{1,0:T(8,128)} %off_h.1, ...), custom_call_target="tpu_custom_call" | custom-call | tf_op jit(solution)/shard_map/sensitivity/pallas_call | solution.py:437
  48.0 0.0 copy-start
  48.0 3.2 %copy.13 = f32[64,64,128]{2,1,0:T(8,128)} copy(f32[64,64,128]{2,1,0:T(8,128)} %get-tuple-element.8) | data formatting | bytes 4194304
  51.2 0.0 copy-done
  51.2 0.6 %copy.14 = f32[1024]{0:T(1024)} copy(f32[1024]{0:T(1024)S(1)} %bitcast.6) | data formatting | bytes 8192
Async XLA Ops:
  48.0 3.2 %copy-start = (f32[1,1024]{1,0:T(1,128)S(1)}, f32[1,1024]{1,0:T(1,128)}, u32[]{:S(2)}) copy-start(f32[1,1024]{1,0:T(1,128)} %get-tuple-element.5) | copy-start | bytes 12292

commit v7 on v5

--- a/solution.py
+++ b/solution.py
@@ -154,6 +154,23 @@
     is_p = jlane == (jrow + 4) % 8
     msend[...] = jnp.where(is_id, id_rows, jnp.where(is_p, p_rows, 0.0))
 
+    def row_copy(src, dst, send_sem, recv_sem, to):
+        return pltpu.make_async_remote_copy(
+            src_ref=src, dst_ref=dst, send_sem=send_sem, recv_sem=recv_sem,
+            device_id=to, device_id_type=MESH,
+        )
+
+    def greeted_and_told():
+        pl.semaphore_wait(barrier, ndev - 1)
+
+        pltpu.make_async_copy(msend.at[pl.ds(0, 1)], mrecv.at[pl.ds(0, 1)], mrsem).start()
+
+        def send_meta(g, m):
+            row = pl.ds(g * gsrc + m, 1)
+            row_copy(msend.at[row], mrecv.at[row], msem, mrsem, ahead(g, m)).start()
+
+        others_in_turn(send_meta, 0, groups)
+
     loads[2].wait()
     loads[3].wait()
     entries = off.shape[0]
@@ -161,6 +178,8 @@
     sub = iota((8, LANES), 0)
     for b in range(blocks):
         sl = slice(b * LANES, (b + 1) * LANES)
+        if b == blocks - 2:
+            greeted_and_told()
 
         @pl.loop(0, entries // 8, unroll=2)
         def _(i):
@@ -190,22 +209,6 @@
         hi, lo = split2(built.T)
         wt[sl, 0:LANES] = hi
         wt[sl, LANES : 2 * LANES] = lo
-
-    pl.semaphore_wait(barrier, ndev - 1)
-
-    def row_copy(src, dst, send_sem, recv_sem, to):
-        return pltpu.make_async_remote_copy(
-            src_ref=src, dst_ref=dst, send_sem=send_sem, recv_sem=recv_sem,
-            device_id=to, device_id_type=MESH,
-        )
-
-    pltpu.make_async_copy(msend.at[pl.ds(0, 1)], mrecv.at[pl.ds(0, 1)], mrsem).start()
-
-    def send_meta(g, m):
-        row = pl.ds(g * gsrc + m, 1)
-        row_copy(msend.at[row], mrecv.at[row], msem, mrsem, ahead(g, m)).start()
-
-    others_in_turn(send_meta, 0, groups)
 
     def send_maps(g, m):
         at = pl.ds(pl.multiple_of((g * gsrc + m) * CAP, CAP), CAP)

time: 48.2 us -> 48.1 us (level)
  no operation moved by 1% of the time
where the time goes in v7:
time: 48.1 us; the launch traced here: 48 us
  Pallas kernels  43.6 us (91%)
  local copies, waits for them, and re-layouts  3.76 us (8%)
  between operations  0.65 us (1%)
    pallas_call x1, Pallas kernels, body(): pl.pallas_call(functools.partial(kernel, nb, nd, wx, wy), out_shape=(jax....  43.6 us
    unnamed x4, local copies, waits for them, and re-layouts  3.76 us

profile of v7, /device:TPU:1, one launch (start us, length us, event | category | flops | bytes accessed | tf_op | source)
XLA Modules:
  0.0 48.0 jit_solution(14617566334094990587)
XLA Ops:
  0.6 43.6 %sensitivity.1 = (f32[64,64,128]{2,1,0:T(8,128)}, f32[1,1024]{1,0:T(1,128)}) custom-call(bf16[27,27]{1,0:T(8,128)(2,1)} %coup_h.1, f32[1,1024]{1,0:T(1,128)} %bitcast.7, s32[1,1024]{1,0:T(1,128)} %bitcast.8, s32[1,1024]{1,0:T(1,128)} %bitcast.9, bf16[3,27,1024]{2,1,0:T(8,128)(2,1)} %vel_h.1, bf16[3,27,1024]{2,1,0:T(8,128)(2,1)} %adj_h.1, s32[128,1024]{1,0:T(8,128)} %off_h.1, ...), custom_call_target="tpu_custom_call" | custom-call | tf_op jit(solution)/shard_map/sensitivity/pallas_call | solution.py:436
  44.2 0.0 copy-start
  44.2 3.2 %copy.13 = f32[64,64,128]{2,1,0:T(8,128)} copy(f32[64,64,128]{2,1,0:T(8,128)} %get-tuple-element.8) | data formatting | bytes 4194304
  47.4 0.0 copy-done
  47.4 0.6 %copy.14 = f32[1024]{0:T(1024)} copy(f32[1024]{0:T(1024)S(1)} %bitcast.6) | data formatting | bytes 8192
Async XLA Ops:
  44.2 3.2 %copy-start = (f32[1,1024]{1,0:T(1,128)S(1)}, f32[1,1024]{1,0:T(1,128)}, u32[]{:S(2)}) copy-start(f32[1,1024]{1,0:T(1,128)} %get-tuple-element.5) | copy-start | bytes 12292
